TPU v7x, 768 devices: a whole 4x8x12 slice. The times are simulated.
768 devices in a mesh: space: 192 (over x_lo, z, y), tracer: 4 (over x_hi, core).
Axes of the slice: x: 4 (x_hi: 2, x_lo: 2; x = x_hi * 2 + x_lo), y: 8, z: 12, core: 2. Of those that a mesh axis runs over, the one named last changes fastest.
Arguments:
- populations: float32 [19, 1536, 16, 128], P(None, 'space', 'tracer'), may hold values from 0 to 0.5
- solid_mask: int32 [1536, 16, 128], P('space', 'tracer'), may hold values 0 or 1
- tracers: float32 [64, 1536, 16, 128], P('tracer', 'space'), may hold values from 0.05 to 2
- decay_rates: float32 [64], P('tracer'), may hold values from 0.02 to 0.4
- buoyancy_coeffs: float32 [64], P('tracer'), may hold values from -0.04 to 0.04
- source_cells: int32 [64, 8], P('tracer'), may hold values from 0 to 3145727
- source_rates: float32 [64, 8], P('tracer'), may hold values from 0.5 to 4
Outputs:
- populations_out: float32 [19, 1536, 16, 128], P(None, 'space', 'tracer')
- velocity_out: float32 [3, 1536, 16, 128], P(None, 'space', 'tracer')
- tracers_out: float32 [64, 1536, 16, 128], P('tracer', 'space')
All inputs are finite; a program needn't handle non-finite values. No bound on the sum of `solid_mask` on one device may be relied on, other than what follows from the above.
Results may differ from a plain program's by a relative error of at most 0.0003.
Values may be sent and summed in bfloat16 or wider, within the bound.
A program may use at most 32 MiB of HBM per device.

v0:
```python
import jax
import jax.numpy as jnp
from jax import lax
from jax.sharding import PartitionSpec as P

SECTIONS = 2


lattice_dirs = (
    (0, 0, 0),
    (1, 0, 0),
    (-1, 0, 0),
    (0, 1, 0),
    (0, -1, 0),
    (0, 0, 1),
    (0, 0, -1),
    (1, 1, 0),
    (-1, -1, 0),
    (1, -1, 0),
    (-1, 1, 0),
    (1, 0, 1),
    (-1, 0, -1),
    (1, 0, -1),
    (-1, 0, 1),
    (0, 1, 1),
    (0, -1, -1),
    (0, 1, -1),
    (0, -1, 1),
)
lattice_weights = (1.0 / 3.0,) + (1.0 / 18.0,) * 6 + (1.0 / 36.0,) * 12
opposite = (0, 2, 1, 4, 3, 6, 5, 8, 7, 10, 9, 12, 11, 14, 13, 16, 15, 18, 17)
relax_rate = 1.25


def padded_2(cells, sides, width):
    for axis, dim in sides:
        count = lax.axis_size(axis)
        ends = count - 1
        head = lax.slice_in_dim(cells, 0, width, axis=dim)
        tail = lax.slice_in_dim(cells, cells.shape[dim] - width, cells.shape[dim], axis=dim)
        cells = jnp.concatenate(
            [
                lax.ppermute(tail, axis, [(i, (i + 1) % count) for i in range(ends)]),
                cells,
                lax.ppermute(head, axis, [((i + 1) % count, i) for i in range(ends)]),
            ],
            axis=dim,
        )
    return cells


def moments(lattice):
    density = jnp.sum(lattice, axis=0)
    velocity_parts = []
    for axis_num in range(3):
        total = jnp.zeros_like(density)
        for direction in range(19):
            component = lattice_dirs[direction][axis_num]
            if component != 0:
                total = total + component * lattice[direction]
        velocity_parts.append(total / density)
    return (density, jnp.stack(velocity_parts))


def collide(lattice, force):
    density, velocity = moments(lattice)
    speed_sq = velocity[0] * velocity[0] + velocity[1] * velocity[1] + velocity[2] * velocity[2]
    posts = []
    for direction in range(19):
        offsets = lattice_dirs[direction]
        weight = lattice_weights[direction]
        along = offsets[0] * velocity[0] + offsets[1] * velocity[1] + offsets[2] * velocity[2]
        equal = weight * density * (1.0 + 3.0 * along + 4.5 * along * along - 1.5 * speed_sq)
        posts.append(
            lattice[direction]
            - relax_rate * (lattice[direction] - equal)
            + 3.0 * weight * offsets[2] * force
        )
    return jnp.stack(posts)


def stream(padded, post, fluid):
    span_x, span_y, span_z = (post.shape[1], post.shape[2], post.shape[3])
    fresh = []
    for direction in range(19):
        offsets = lattice_dirs[direction]
        low_x, low_y, low_z = (1 - offsets[0], 1 - offsets[1], 1 - offsets[2])
        neighbour = padded[
            direction, low_x : low_x + span_x, low_y : low_y + span_y, low_z : low_z + span_z
        ]
        open_side = padded[
            19, low_x : low_x + span_x, low_y : low_y + span_y, low_z : low_z + span_z
        ]
        bounced = post[opposite[direction]]
        fresh.append(
            fluid * (open_side * neighbour + (1.0 - open_side) * bounced)
            + (1.0 - fluid) * post[direction]
        )
    return jnp.stack(fresh)


def lattice_step(lattice, fluid, force):
    post = collide(lattice, force)
    payload = jnp.concatenate([post, fluid[None]], axis=0)
    padded = padded_2(payload, (("space", 1), ("tracer", 2)), 1)
    padded = jnp.pad(padded, ((0, 0), (0, 0), (0, 0), (1, 1)))
    return stream(padded, post, fluid)


def window(array, axis_num, start, count):
    return lax.slice_in_dim(array, start, start + count, axis=axis_num)


def minmod(first, second):
    return 0.5 * (jnp.sign(first) + jnp.sign(second)) * jnp.minimum(jnp.abs(first), jnp.abs(second))


def face_flux(conc, speed, fluid, axis_num):
    count = conc.shape[axis_num] - 4
    behind = window(conc, axis_num, 0, count + 1)
    current = window(conc, axis_num, 1, count + 1)
    ahead_one = window(conc, axis_num, 2, count + 1)
    ahead_two = window(conc, axis_num, 3, count + 1)
    left_state = current + 0.5 * minmod(current - behind, ahead_one - current)
    right_state = ahead_one - 0.5 * minmod(ahead_one - current, ahead_two - ahead_one)
    face_speed = 0.5 * (
        window(speed, axis_num, 1, count + 1) + window(speed, axis_num, 2, count + 1)
    )
    face_speed = (
        face_speed * window(fluid, axis_num, 1, count + 1) * window(fluid, axis_num, 2, count + 1)
    )
    flux = jnp.maximum(face_speed, 0.0) * left_state + jnp.minimum(face_speed, 0.0) * right_state
    return window(flux, axis_num, 1, count) - window(flux, axis_num, 0, count)


def tracer_section(conc, flow, rates, emission):
    count = conc.shape[1] - 4

    def inner(array):
        return window(array, 1, 2, count)

    def pad_side(array, axis_num):
        widths = [(0, 0)] * 4
        widths[axis_num] = (2, 2)
        return jnp.pad(array, widths)

    air = flow[3:4]
    div_x = face_flux(conc, flow[0:1], air, 1)
    div_y = face_flux(
        pad_side(inner(conc), 2), pad_side(inner(flow[1:2]), 2), pad_side(inner(air), 2), 2
    )
    div_z = face_flux(
        pad_side(inner(conc), 3), pad_side(inner(flow[2:3]), 3), pad_side(inner(air), 3), 3
    )
    center = inner(conc)
    rate_col = rates[:, None, None, None]
    lost = rate_col * center
    paired = lost.reshape((lost.shape[0] // 2, 2) + lost.shape[1:])
    produced = jnp.stack([jnp.zeros_like(paired[:, 0]), paired[:, 0]], axis=1).reshape(center.shape)
    return center + (produced - lost - (div_x + div_y + div_z) + emission)


def local(
    populations, solid_mask, tracers, decay_rates, buoyancy_coeffs, source_cells, source_rates
):
    fluid = 1.0 - solid_mask.astype(jnp.float32)
    lattice = populations
    for turn in range(2):
        lattice = lattice_step(lattice, fluid, 0.0)
    density, velocity = moments(lattice)
    flow = jnp.concatenate([velocity * fluid, fluid[None]], axis=0).astype(jnp.bfloat16)
    whole_flow = lax.all_gather(flow, "tracer", axis=2, tiled=True)
    flow_wide = whole_flow.astype(jnp.float32)
    group = tracers.shape[0]
    span_x, span_y, span_z = (tracers.shape[1], tracers.shape[2], tracers.shape[3])
    margin_max = 2
    reach = span_x + 2 * (margin_max - 2)
    first_x = lax.axis_index("space") * span_x - (margin_max - 2)
    global_x = first_x + jnp.arange(reach)
    flat_cells = (global_x[:, None, None] * span_y + jnp.arange(span_y)[None, :, None]) * span_z
    flat_cells = flat_cells + jnp.arange(span_z)[None, None, :]
    emission = jnp.zeros((group, reach, span_y, span_z), jnp.float32)
    for source_num in range(source_cells.shape[1]):
        hits = (flat_cells[None] == source_cells[:, source_num, None, None, None]).astype(
            jnp.float32
        )
        emission = emission + source_rates[:, source_num, None, None, None] * hits
    current = tracers
    margin = 0
    flow_ext = flow_wide
    for section in range(SECTIONS):
        joined = padded_2(
            jnp.concatenate([current, flow_wide], axis=0), (("space", 1),), margin_max
        )
        current = joined[:group]
        flow_ext = joined[group:]
        margin = margin_max
        flow_now = window(flow_ext, 1, margin_max - margin, span_x + 2 * margin)
        emit_now = window(emission, 1, margin_max - margin, span_x + 2 * margin - 4)
        current = tracer_section(current, flow_now, decay_rates, emit_now)
        margin = margin - 2
    partial_value = jnp.einsum(
        "t,txyz->xyz", buoyancy_coeffs, current, precision=lax.Precision.HIGHEST
    )
    force = lax.psum_scatter(partial_value, "tracer", scatter_dimension=1, tiled=True)
    lattice = lattice_step(lattice, fluid, force)
    density, velocity = moments(lattice)
    return (lattice, velocity * fluid, current)


def solution(mesh):
    placed = (
        P(None, "space", "tracer", None),
        P("space", "tracer", None),
        P("tracer", "space", None, None),
        P("tracer"),
        P("tracer"),
        P("tracer", None),
        P("tracer", None),
    )
    return jax.shard_map(
        local,
        mesh=mesh,
        in_specs=placed,
        out_specs=(
            P(None, "space", "tracer", None),
            P(None, "space", "tracer", None),
            P("tracer", "space", None, None),
        ),
        check_vma=False,
    )
```

profile of v0, /device:TPU:1, one launch (start us, length us, event | category | flops | bytes accessed | tf_op | source)
XLA Modules:
  0.0 199.3 jit_solution(4832275329505319462)
XLA Ops:
  7.2 0.9 fusion.944
  8.2 1.0 reduce_sum.189
  9.2 0.2 constant_dynamic-update-slice_fusion.19
  10.0 4.0 %collective-permute-start = (f32[20,1,4,128]{3,1,2,0:T(1,128)S(1)}, f32[20,1,4,128]{3,1,2,0:T(1,128)S(1)}, u32[]{:S(2)}, u32[]{:S(2)}) collective-permute-start(f32[20,1,4,128]{3,1,2,0:T(1,128)S(1)} %get-tuple-element.189), channel_id=1, source_target_pairs={{0,4},{4,8},{8,12},{12,16},{16,20},{20,24},{24,28},{28,32},{32,36}... | collective-permute-start | bytes 122888 | tf_op jit(solution)/shard_map/ppermute | solution.py:43
  14.0 1.3 collective-permute-start.1
  15.5 0.8 fusion.258
  16.2 0.6 fusion.264
  17.1 1.6 collective-permute-done.1
  18.9 6.8 %collective-permute-start.2 = (f32[20,10,1,128]{3,1,2,0:T(8,128)S(1)}, f32[20,10,1,128]{3,1,2,0:T(8,128)S(1)}, u32[]{:S(2)}, u32[]{:S(2)}) collective-permute-start(f32[20,10,1,128]{3,1,2,0:T(8,128)S(1)} %get-tuple-element.183), channel_id=1, source_target_pairs={{0,1},{1,2},{2,3},{4,5},{5,6},{6,7},{8,9},{9,10},{10,11},{12,13},{... | collective-permute-start | bytes 307208 | tf_op jit(solution)/shard_map/ppermute | solution.py:43
  25.7 5.5 %collective-permute-start.3 = (f32[20,10,1,128]{3,1,2,0:T(8,128)S(1)}, f32[20,10,1,128]{3,1,2,0:T(8,128)S(1)}, u32[]{:S(2)}, u32[]{:S(2)}) collective-permute-start(f32[20,10,1,128]{3,1,2,0:T(8,128)S(1)} %get-tuple-element.182), channel_id=1, source_target_pairs={{1,0},{2,1},{3,2},{5,4},{6,5},{7,6},{9,8},{10,9},{11,10},{13,12},{... | collective-permute-start | bytes 307208 | tf_op jit(solution)/shard_map/ppermute | solution.py:45
  31.2 3.0 %collective-permute-done.3 = f32[20,10,1,128]{3,1,2,0:T(8,128)S(1)} collective-permute-done((f32[20,10,1,128]{3,1,2,0:T(8,128)S(1)}, f32[20,10,1,128]{3,1,2,0:T(8,128)S(1)}, u32[]{:S(2)}, u32[]{:S(2)}) %collective-permute-start.3) | collective-permute-done | bytes 102432 | tf_op jit(solution)/shard_map/ppermute | solution.py:45
  34.3 0.9 select_maximum_fusion.8
  35.3 0.2 constant_dynamic-update-slice_fusion.39
  36.1 2.8 %collective-permute-start.4 = (f32[20,1,4,128]{3,1,2,0:T(1,128)S(1)}, f32[20,1,4,128]{3,1,2,0:T(1,128)S(1)}, u32[]{:S(2)}, u32[]{:S(2)}) collective-permute-start(f32[20,1,4,128]{3,1,2,0:T(1,128)S(1)} %get-tuple-element.187), channel_id=1, source_target_pairs={{0,4},{4,8},{8,12},{12,16},{16,20},{20,24},{24,28},{28,32},{32,36}... | collective-permute-start | bytes 122888 | tf_op jit(solution)/shard_map/ppermute | solution.py:43
  38.8 1.3 collective-permute-start.5
  40.2 4.0 %collective-permute-done.5 = f32[20,1,4,128]{3,1,2,0:T(1,128)S(1)} collective-permute-done((f32[20,1,4,128]{3,1,2,0:T(1,128)S(1)}, f32[20,1,4,128]{3,1,2,0:T(1,128)S(1)}, u32[]{:S(2)}, u32[]{:S(2)}) %collective-permute-start.5) | collective-permute-done | bytes 40992 | tf_op jit(solution)/shard_map/ppermute | solution.py:45
  44.3 2.9 %collective-permute-start.6 = (f32[20,10,1,128]{3,1,2,0:T(8,128)S(1)}, f32[20,10,1,128]{3,1,2,0:T(8,128)S(1)}, u32[]{:S(2)}, u32[]{:S(2)}) collective-permute-start(f32[20,10,1,128]{3,1,2,0:T(8,128)S(1)} %get-tuple-element.181), channel_id=1, source_target_pairs={{0,1},{1,2},{2,3},{4,5},{5,6},{6,7},{8,9},{9,10},{10,11},{12,13},{... | collective-permute-start | bytes 307208 | tf_op jit(solution)/shard_map/ppermute | solution.py:43
  47.2 1.9 collective-permute-start.7
  49.4 5.9 %collective-permute-done.7 = f32[20,10,1,128]{3,1,2,0:T(8,128)S(1)} collective-permute-done((f32[20,10,1,128]{3,1,2,0:T(8,128)S(1)}, f32[20,10,1,128]{3,1,2,0:T(8,128)S(1)}, u32[]{:S(2)}, u32[]{:S(2)}) %collective-permute-start.7) | collective-permute-done | bytes 102432 | tf_op jit(solution)/shard_map/ppermute | solution.py:45
  55.3 0.9 select_maximum_fusion.4
  56.2 0.8 add_divide_fusion.2
  57.2 5.8 %all_gather.3 = bf16[4,8,16,128]{3,1,0,2:T(8,128)(2,1)S(1)} all-gather(bf16[4,8,4,128]{3,1,0,2:T(8,128)(2,1)S(1)} %copy.131), channel_id=1, replica_groups=mesh['space'=192,'tracer'=4] {'tracer'}, dimensions={2}, use_global_device_ids=true | all-gather | bytes 163840 | tf_op jit(solution)/shard_map/all_gather | solution.py:172
  63.4 4.9 %collective-permute-start.8 = (f32[20,2,16,128]{3,2,1,0:T(8,128)S(1)}, f32[20,2,16,128]{3,2,1,0:T(8,128)S(1)}, u32[]{:S(2)}, u32[]{:S(2)}) collective-permute-start(f32[20,2,16,128]{3,2,1,0:T(8,128)S(1)} %get-tuple-element.174), channel_id=1, source_target_pairs={{0,4},{4,8},{8,12},{12,16},{16,20},{20,24},{24,28},{28,32},{32,36}... | collective-permute-start | bytes 983048 | tf_op jit(solution)/shard_map/ppermute | solution.py:43
  68.3 1.5 collective-permute-start.9
  70.1 2.8 %multiply_add_fusion.1 = f32[16,8,16,129]{3,2,1,0:T(8,128)S(1)} fusion(f32[16,8,16,128]{3,2,1,0:T(8,128)S(1)} %copy-done.1, f32[8,16,129]{2,1,0:T(8,128)S(1)} %copy.136, f32[8,16,129]{2,1,0:T(8,128)S(1)} %copy.135), kind=kLoop, calls=%fused_computation.15 | loop fusion | flops 6340608 | bytes 2237440 | tf_op jit(solution)/shard_map/add | solution.py:132
  73.0 2.2 %multiply_add_fusion.3 = f32[16,8,17,128]{3,2,1,0:T(8,128)S(1)} fusion(f32[16,8,16,128]{3,2,1,0:T(8,128)S(1)} %copy-done.1, f32[8,17,128]{2,1,0:T(8,128)S(1)} %copy.134, f32[8,17,128]{2,1,0:T(8,128)S(1)} %copy.133), kind=kLoop, calls=%fused_computation.48 | loop fusion | flops 6684672 | bytes 2301952 | tf_op jit(solution)/shard_map/add | solution.py:132
  75.2 4.1 %collective-permute-done.9 = f32[20,2,16,128]{3,2,1,0:T(8,128)S(1)} collective-permute-done((f32[20,2,16,128]{3,2,1,0:T(8,128)S(1)}, f32[20,2,16,128]{3,2,1,0:T(8,128)S(1)}, u32[]{:S(2)}, u32[]{:S(2)}) %collective-permute-start.9) | collective-permute-done | bytes 327712 | tf_op jit(solution)/shard_map/ppermute | solution.py:45
  79.4 1.6 multiply_add_fusion.5
  81.0 2.1 %broadcast_multiply_fusion = (f32[16,8,16,128]{3,2,1,0:T(8,128)S(1)}, f32[16,8,16,128]{3,2,1,0:T(8,128)S(1)}) fusion(f32[16]{0:T(128)S(1)} %copy-done.46, f32[16,8,16,128]{3,2,1,0:T(8,128)S(1)} %copy-done.1, f32[16]{0:T(128)S(1)} %get-tuple-element.252, s32[16]{0:T(128)S(1)} %get-tuple-element.244, f32[16]{0:T(128)S(1)} %get-tuple-element.253, ...), kind=kLoop, calls=%fused_computation.80 | loop fusion | flops 8912896 | bytes 10552384 | tf_op jit(solution)/shard_map/mul | solution.py:157
  83.1 2.8 %multiply_add_fusion = f32[16,8,16,129]{3,2,1,0:T(8,128)S(1)} fusion(f32[16,8,16,128]{3,2,1,0:T(8,128)S(1)} %get-tuple-element.69, f32[8,16,129]{2,1,0:T(8,128)S(1)} %copy.136, f32[8,16,129]{2,1,0:T(8,128)S(1)} %copy.135), kind=kLoop, calls=%fused_computation.14 | loop fusion | flops 6340608 | bytes 2237440 | tf_op jit(solution)/shard_map/add | solution.py:132
  86.0 3.1 %collective-permute-start.10 = (f32[20,2,16,128]{3,2,1,0:T(8,128)S(1)}, f32[20,2,16,128]{3,2,1,0:T(8,128)S(1)}, u32[]{:S(2)}, u32[]{:S(2)}) collective-permute-start(f32[20,2,16,128]{3,2,1,0:T(8,128)S(1)} %get-tuple-element.172), channel_id=1, source_target_pairs={{0,4},{4,8},{8,12},{12,16},{16,20},{20,24},{24,28},{28,32},{32,36}... | collective-permute-start | bytes 983048 | tf_op jit(solution)/shard_map/ppermute | solution.py:43
  89.1 1.5 collective-permute-start.11
  90.8 2.2 %multiply_add_fusion.2 = f32[16,8,17,128]{3,2,1,0:T(8,128)S(1)} fusion(f32[16,8,16,128]{3,2,1,0:T(8,128)S(1)} %get-tuple-element.69, f32[8,17,128]{2,1,0:T(8,128)S(1)} %copy.134, f32[8,17,128]{2,1,0:T(8,128)S(1)} %copy.133), kind=kLoop, calls=%fused_computation.47 | loop fusion | flops 6684672 | bytes 2301952 | tf_op jit(solution)/shard_map/add | solution.py:132
  93.0 1.6 collective-permute-done.10
  94.7 3.9 %collective-permute-done.11 = f32[20,2,16,128]{3,2,1,0:T(8,128)S(1)} collective-permute-done((f32[20,2,16,128]{3,2,1,0:T(8,128)S(1)}, f32[20,2,16,128]{3,2,1,0:T(8,128)S(1)}, u32[]{:S(2)}, u32[]{:S(2)}) %collective-permute-start.11) | collective-permute-done | bytes 327712 | tf_op jit(solution)/shard_map/ppermute | solution.py:45
  98.6 0.4 maximum_maximum_fusion
  98.9 1.6 multiply_add_fusion.4
  100.6 1.9 fusion.16
  102.6 1.3 fusion.23
  103.9 0.7 copy.562
  104.6 55.1 %reduce-scatter.2.cloned.1.call-done = f32[8,4,128]{2,0,1:T(8,128)} async-done(((f32[8,16,128]{2,0,1:T(8,128)}), f32[8,4,128]{2,0,1:T(8,128)}) %reduce-scatter.2.cloned.1.call-update) | async-done | bytes 16400 | tf_op jit(solution)/shard_map/reduce_scatter | solution.py:205
  159.7 0.8 constant_dynamic-update-slice_fusion.61
  160.5 0.7 constant_dynamic-update-slice_fusion.60
  161.3 0.7 constant_dynamic-update-slice_fusion.59
  162.0 0.7 constant_dynamic-update-slice_fusion.58
  162.8 0.7 constant_dynamic-update-slice_fusion.57
  163.5 0.7 constant_dynamic-update-slice_fusion.56
  164.3 0.7 constant_dynamic-update-slice_fusion.55
  165.0 0.7 constant_dynamic-update-slice_fusion.54
  165.8 0.7 constant_dynamic-update-slice_fusion.53
  166.5 0.7 constant_dynamic-update-slice_fusion.52
  167.3 0.7 constant_dynamic-update-slice_fusion.51
  168.4 3.1 %collective-permute-start.12 = (f32[20,1,4,128]{3,1,2,0:T(1,128)S(1)}, f32[20,1,4,128]{3,1,2,0:T(1,128)S(1)}, u32[]{:S(2)}, u32[]{:S(2)}) collective-permute-start(f32[20,1,4,128]{3,1,2,0:T(1,128)S(1)} %get-tuple-element.184), channel_id=1, source_target_pairs={{0,4},{4,8},{8,12},{12,16},{16,20},{20,24},{24,28},{28,32},{32,36}... | collective-permute-start | bytes 122888 | tf_op jit(solution)/shard_map/ppermute | solution.py:43
  171.5 1.3 collective-permute-start.13
  172.8 3.4 %collective-permute-done.13 = f32[20,1,4,128]{3,1,2,0:T(1,128)S(1)} collective-permute-done((f32[20,1,4,128]{3,1,2,0:T(1,128)S(1)}, f32[20,1,4,128]{3,1,2,0:T(1,128)S(1)}, u32[]{:S(2)}, u32[]{:S(2)}) %collective-permute-start.13) | collective-permute-done | bytes 40992 | tf_op jit(solution)/shard_map/ppermute | solution.py:45
  176.3 4.7 %collective-permute-start.14 = (f32[20,10,1,128]{3,1,2,0:T(8,128)S(1)}, f32[20,10,1,128]{3,1,2,0:T(8,128)S(1)}, u32[]{:S(2)}, u32[]{:S(2)}) collective-permute-start(f32[20,10,1,128]{3,1,2,0:T(8,128)S(1)} %get-tuple-element.178), channel_id=1, source_target_pairs={{0,1},{1,2},{2,3},{4,5},{5,6},{6,7},{8,9},{9,10},{10,11},{12,13},{... | collective-permute-start | bytes 307208 | tf_op jit(solution)/shard_map/ppermute | solution.py:43
  181.0 1.9 collective-permute-start.15
  183.0 0.3 collective-permute-done.14
  183.3 5.9 %collective-permute-done.15 = f32[20,10,1,128]{3,1,2,0:T(8,128)S(1)} collective-permute-done((f32[20,10,1,128]{3,1,2,0:T(8,128)S(1)}, f32[20,10,1,128]{3,1,2,0:T(8,128)S(1)}, u32[]{:S(2)}, u32[]{:S(2)}) %collective-permute-start.15) | collective-permute-done | bytes 102432 | tf_op jit(solution)/shard_map/ppermute | solution.py:45
  189.2 0.9 select_maximum_fusion
  190.1 0.2 divide_bitcast_fusion.2
  190.4 0.5 copy-done.34
  190.8 0.6 copy.139
  191.7 0.8 copy.138
  (211 shorter events, 3.2 us)
Async XLA Ops:
  7.2 95.3 %copy-start = (f32[16]{0:T(128)S(1)}, f32[16]{0:T(128)}, u32[]{:S(2)}) copy-start(f32[16]{0:T(128)} %param.11) | copy-start | bytes 196
  7.2 152.5 %reduce-scatter.2.cloned.1.call-start = ((), (), s32[]{:S(2)}) async-start(), calls=%async_computation.1 | async-start | bytes 81920 | tf_op jit(solution)/shard_map/reduce_scatter | solution.py:205
  9.5 7.4 %copy-start.1 = (f32[16,8,16,128]{3,2,1,0:T(8,128)S(1)}, f32[16,8,16,128]{3,2,1,0:T(8,128)}, u32[]{:S(2)}) copy-start(f32[16,8,16,128]{3,2,1,0:T(8,128)} %param.9) | copy-start | bytes 3145732
  9.5 7.4 %copy-start.46 = (f32[16]{0:T(128)S(1)}, f32[16]{0:T(128)}, u32[]{:S(2)}) copy-start(f32[16]{0:T(128)} %param.10) | copy-start | bytes 196
  10.0 7.2 %collective-permute-start = (f32[20,1,4,128]{3,1,2,0:T(1,128)S(1)}, f32[20,1,4,128]{3,1,2,0:T(1,128)S(1)}, u32[]{:S(2)}, u32[]{:S(2)}) collective-permute-start(f32[20,1,4,128]{3,1,2,0:T(1,128)S(1)} %get-tuple-element.189), channel_id=1, source_target_pairs={{0,4},{4,8},{8,12},{12,16},{16,20},{20,24},{24,28},{28,32},{32,36}... | collective-permute-start | bytes 122888 | tf_op jit(solution)/shard_map/ppermute | solution.py:43
  14.0 4.7 %collective-permute-start.1 = (f32[20,1,4,128]{3,1,2,0:T(1,128)S(1)}, f32[20,1,4,128]{3,1,2,0:T(1,128)S(1)}, u32[]{:S(2)}, u32[]{:S(2)}) collective-permute-start(f32[20,1,4,128]{3,1,2,0:T(1,128)S(1)} %get-tuple-element.188), channel_id=1, source_target_pairs={{4,0},{8,4},{12,8},{16,12},{20,16},{24,20},{28,24},{32,28},{36,32}... | collective-permute-start | bytes 122888 | tf_op jit(solution)/shard_map/ppermute | solution.py:45
  16.9 40.3 %copy-start.33 = (f32[8,4,128]{2,0,1:T(8,128)}, f32[8,4,128]{2,0,1:T(8,128)S(1)}, u32[]{:S(2)}) copy-start(f32[8,4,128]{2,0,1:T(8,128)S(1)} %get-tuple-element.234) | copy-start | bytes 49156
  18.8 16.4 %copy-start.37 = (f32[8,4,128]{2,0,1:T(8,128)S(1)}, f32[8,4,128]{2,0,1:T(8,128)}, u32[]{:S(2)}) copy-start(f32[8,4,128]{2,0,1:T(8,128)} %get-tuple-element.225) | copy-start | bytes 49156
  18.8 16.4 %copy-start.38 = (f32[8,4,128]{2,0,1:T(8,128)S(1)}, f32[8,4,128]{2,0,1:T(8,128)}, u32[]{:S(2)}) copy-start(f32[8,4,128]{2,0,1:T(8,128)} %get-tuple-element.226) | copy-start | bytes 49156
  18.8 16.4 %copy-start.39 = (f32[8,4,128]{2,0,1:T(8,128)S(1)}, f32[8,4,128]{2,0,1:T(8,128)}, u32[]{:S(2)}) copy-start(f32[8,4,128]{2,0,1:T(8,128)} %get-tuple-element.227) | copy-start | bytes 49156
  18.8 16.4 %copy-start.40 = (f32[8,4,128]{2,0,1:T(8,128)S(1)}, f32[8,4,128]{2,0,1:T(8,128)}, u32[]{:S(2)}) copy-start(f32[8,4,128]{2,0,1:T(8,128)} %get-tuple-element.228) | copy-start | bytes 49156
  18.8 16.4 %copy-start.41 = (f32[8,4,128]{2,0,1:T(8,128)S(1)}, f32[8,4,128]{2,0,1:T(8,128)}, u32[]{:S(2)}) copy-start(f32[8,4,128]{2,0,1:T(8,128)} %get-tuple-element.229) | copy-start | bytes 49156
  18.8 16.4 %copy-start.42 = (f32[8,4,128]{2,0,1:T(8,128)S(1)}, f32[8,4,128]{2,0,1:T(8,128)}, u32[]{:S(2)}) copy-start(f32[8,4,128]{2,0,1:T(8,128)} %get-tuple-element.230) | copy-start | bytes 49156
  18.9 16.4 %copy-start.43 = (f32[8,4,128]{2,0,1:T(8,128)S(1)}, f32[8,4,128]{2,0,1:T(8,128)}, u32[]{:S(2)}) copy-start(f32[8,4,128]{2,0,1:T(8,128)} %get-tuple-element.231) | copy-start | bytes 49156
  18.9 16.4 %copy-start.44 = (f32[8,4,128]{2,0,1:T(8,128)S(1)}, f32[8,4,128]{2,0,1:T(8,128)}, u32[]{:S(2)}) copy-start(f32[8,4,128]{2,0,1:T(8,128)} %get-tuple-element.232) | copy-start | bytes 49156
  18.9 16.4 %copy-start.45 = (f32[8,4,128]{2,0,1:T(8,128)S(1)}, f32[8,4,128]{2,0,1:T(8,128)}, u32[]{:S(2)}) copy-start(f32[8,4,128]{2,0,1:T(8,128)} %get-tuple-element.233) | copy-start | bytes 49156
  18.9 12.3 %collective-permute-start.2 = (f32[20,10,1,128]{3,1,2,0:T(8,128)S(1)}, f32[20,10,1,128]{3,1,2,0:T(8,128)S(1)}, u32[]{:S(2)}, u32[]{:S(2)}) collective-permute-start(f32[20,10,1,128]{3,1,2,0:T(8,128)S(1)} %get-tuple-element.183), channel_id=1, source_target_pairs={{0,1},{1,2},{2,3},{4,5},{5,6},{6,7},{8,9},{9,10},{10,11},{12,13},{... | collective-permute-start | bytes 307208 | tf_op jit(solution)/shard_map/ppermute | solution.py:43
  25.7 8.6 %collective-permute-start.3 = (f32[20,10,1,128]{3,1,2,0:T(8,128)S(1)}, f32[20,10,1,128]{3,1,2,0:T(8,128)S(1)}, u32[]{:S(2)}, u32[]{:S(2)}) collective-permute-start(f32[20,10,1,128]{3,1,2,0:T(8,128)S(1)} %get-tuple-element.182), channel_id=1, source_target_pairs={{1,0},{2,1},{3,2},{5,4},{6,5},{7,6},{9,8},{10,9},{11,10},{13,12},{... | collective-permute-start | bytes 307208 | tf_op jit(solution)/shard_map/ppermute | solution.py:45
  35.5 4.6 %copy-start.47 = (s32[16,8]{0,1:T(8,128)S(1)}, s32[16,8]{0,1:T(8,128)}, u32[]{:S(2)}) copy-start(s32[16,8]{0,1:T(8,128)} %param.12) | copy-start | bytes 1540
  35.6 13.5 %copy-start.48 = (f32[16,8]{0,1:T(8,128)S(1)}, f32[16,8]{0,1:T(8,128)}, u32[]{:S(2)}) copy-start(f32[16,8]{0,1:T(8,128)} %param.13) | copy-start | bytes 1540
  36.1 4.1 %collective-permute-start.4 = (f32[20,1,4,128]{3,1,2,0:T(1,128)S(1)}, f32[20,1,4,128]{3,1,2,0:T(1,128)S(1)}, u32[]{:S(2)}, u32[]{:S(2)}) collective-permute-start(f32[20,1,4,128]{3,1,2,0:T(1,128)S(1)} %get-tuple-element.187), channel_id=1, source_target_pairs={{0,4},{4,8},{8,12},{12,16},{16,20},{20,24},{24,28},{28,32},{32,36}... | collective-permute-start | bytes 122888 | tf_op jit(solution)/shard_map/ppermute | solution.py:43
  38.8 5.4 %collective-permute-start.5 = (f32[20,1,4,128]{3,1,2,0:T(1,128)S(1)}, f32[20,1,4,128]{3,1,2,0:T(1,128)S(1)}, u32[]{:S(2)}, u32[]{:S(2)}) collective-permute-start(f32[20,1,4,128]{3,1,2,0:T(1,128)S(1)} %get-tuple-element.186), channel_id=1, source_target_pairs={{4,0},{8,4},{12,8},{16,12},{20,16},{24,20},{28,24},{32,28},{36,32}... | collective-permute-start | bytes 122888 | tf_op jit(solution)/shard_map/ppermute | solution.py:45
  44.3 5.1 %collective-permute-start.6 = (f32[20,10,1,128]{3,1,2,0:T(8,128)S(1)}, f32[20,10,1,128]{3,1,2,0:T(8,128)S(1)}, u32[]{:S(2)}, u32[]{:S(2)}) collective-permute-start(f32[20,10,1,128]{3,1,2,0:T(8,128)S(1)} %get-tuple-element.181), channel_id=1, source_target_pairs={{0,1},{1,2},{2,3},{4,5},{5,6},{6,7},{8,9},{9,10},{10,11},{12,13},{... | collective-permute-start | bytes 307208 | tf_op jit(solution)/shard_map/ppermute | solution.py:43
  47.2 8.1 %collective-permute-start.7 = (f32[20,10,1,128]{3,1,2,0:T(8,128)S(1)}, f32[20,10,1,128]{3,1,2,0:T(8,128)S(1)}, u32[]{:S(2)}, u32[]{:S(2)}) collective-permute-start(f32[20,10,1,128]{3,1,2,0:T(8,128)S(1)} %get-tuple-element.180), channel_id=1, source_target_pairs={{1,0},{2,1},{3,2},{5,4},{6,5},{7,6},{9,8},{10,9},{11,10},{13,12},{... | collective-permute-start | bytes 307208 | tf_op jit(solution)/shard_map/ppermute | solution.py:45
  57.0 6.3 %copy-start.5 = (f32[8,4,128]{2,0,1:T(8,128)}, f32[8,4,128]{2,0,1:T(8,128)S(1)}, u32[]{:S(2)}) copy-start(f32[8,4,128]{2,0,1:T(8,128)S(1)} %get-tuple-element.95) | copy-start | bytes 49156
  57.0 6.3 %copy-start.7 = (f32[8,4,128]{2,0,1:T(8,128)}, f32[8,4,128]{2,0,1:T(8,128)S(1)}, u32[]{:S(2)}) copy-start(f32[8,4,128]{2,0,1:T(8,128)S(1)} %get-tuple-element.94) | copy-start | bytes 49156
  57.0 6.3 %copy-start.9 = (f32[8,4,128]{2,0,1:T(8,128)}, f32[8,4,128]{2,0,1:T(8,128)S(1)}, u32[]{:S(2)}) copy-start(f32[8,4,128]{2,0,1:T(8,128)S(1)} %get-tuple-element.93) | copy-start | bytes 49156
  57.0 6.3 %copy-start.11 = (f32[8,4,128]{2,0,1:T(8,128)}, f32[8,4,128]{2,0,1:T(8,128)S(1)}, u32[]{:S(2)}) copy-start(f32[8,4,128]{2,0,1:T(8,128)S(1)} %get-tuple-element.92) | copy-start | bytes 49156
  57.0 6.3 %copy-start.13 = (f32[8,4,128]{2,0,1:T(8,128)}, f32[8,4,128]{2,0,1:T(8,128)S(1)}, u32[]{:S(2)}) copy-start(f32[8,4,128]{2,0,1:T(8,128)S(1)} %get-tuple-element.91) | copy-start | bytes 49156
  57.0 6.3 %copy-start.15 = (f32[8,4,128]{2,0,1:T(8,128)}, f32[8,4,128]{2,0,1:T(8,128)S(1)}, u32[]{:S(2)}) copy-start(f32[8,4,128]{2,0,1:T(8,128)S(1)} %get-tuple-element.90) | copy-start | bytes 49156
  57.0 6.3 %copy-start.17 = (f32[8,4,128]{2,0,1:T(8,128)}, f32[8,4,128]{2,0,1:T(8,128)S(1)}, u32[]{:S(2)}) copy-start(f32[8,4,128]{2,0,1:T(8,128)S(1)} %get-tuple-element.89) | copy-start | bytes 49156
  57.0 6.3 %copy-start.19 = (f32[8,4,128]{2,0,1:T(8,128)}, f32[8,4,128]{2,0,1:T(8,128)S(1)}, u32[]{:S(2)}) copy-start(f32[8,4,128]{2,0,1:T(8,128)S(1)} %get-tuple-element.88) | copy-start | bytes 49156
  57.0 6.3 %copy-start.21 = (f32[8,4,128]{2,0,1:T(8,128)}, f32[8,4,128]{2,0,1:T(8,128)S(1)}, u32[]{:S(2)}) copy-start(f32[8,4,128]{2,0,1:T(8,128)S(1)} %get-tuple-element.87) | copy-start | bytes 49156
  57.1 6.3 %copy-start.23 = (f32[8,4,128]{2,0,1:T(8,128)}, f32[8,4,128]{2,0,1:T(8,128)S(1)}, u32[]{:S(2)}) copy-start(f32[8,4,128]{2,0,1:T(8,128)S(1)} %get-tuple-element.86) | copy-start | bytes 49156
  57.1 6.3 %copy-start.25 = (f32[8,4,128]{2,0,1:T(8,128)}, f32[8,4,128]{2,0,1:T(8,128)S(1)}, u32[]{:S(2)}) copy-start(f32[8,4,128]{2,0,1:T(8,128)S(1)} %get-tuple-element.85) | copy-start | bytes 49156
  57.1 6.3 %copy-start.27 = (f32[8,4,128]{2,0,1:T(8,128)}, f32[8,4,128]{2,0,1:T(8,128)S(1)}, u32[]{:S(2)}) copy-start(f32[8,4,128]{2,0,1:T(8,128)S(1)} %get-tuple-element.84) | copy-start | bytes 49156
  57.1 6.3 %copy-start.29 = (f32[8,4,128]{2,0,1:T(8,128)}, f32[8,4,128]{2,0,1:T(8,128)S(1)}, u32[]{:S(2)}) copy-start(f32[8,4,128]{2,0,1:T(8,128)S(1)} %get-tuple-element.83) | copy-start | bytes 49156
  57.1 6.3 %copy-start.31 = (f32[8,4,128]{2,0,1:T(8,128)}, f32[8,4,128]{2,0,1:T(8,128)S(1)}, u32[]{:S(2)}) copy-start(f32[8,4,128]{2,0,1:T(8,128)S(1)} %get-tuple-element.82) | copy-start | bytes 49156
  63.4 11.8 %collective-permute-start.8 = (f32[20,2,16,128]{3,2,1,0:T(8,128)S(1)}, f32[20,2,16,128]{3,2,1,0:T(8,128)S(1)}, u32[]{:S(2)}, u32[]{:S(2)}) collective-permute-start(f32[20,2,16,128]{3,2,1,0:T(8,128)S(1)} %get-tuple-element.174), channel_id=1, source_target_pairs={{0,4},{4,8},{8,12},{12,16},{16,20},{20,24},{24,28},{28,32},{32,36}... | collective-permute-start | bytes 983048 | tf_op jit(solution)/shard_map/ppermute | solution.py:43
  68.3 11.1 %collective-permute-start.9 = (f32[20,2,16,128]{3,2,1,0:T(8,128)S(1)}, f32[20,2,16,128]{3,2,1,0:T(8,128)S(1)}, u32[]{:S(2)}, u32[]{:S(2)}) collective-permute-start(f32[20,2,16,128]{3,2,1,0:T(8,128)S(1)} %get-tuple-element.175), channel_id=1, source_target_pairs={{4,0},{8,4},{12,8},{16,12},{20,16},{24,20},{28,24},{32,28},{36,32}... | collective-permute-start | bytes 983048 | tf_op jit(solution)/shard_map/ppermute | solution.py:45
  86.0 8.7 %collective-permute-start.10 = (f32[20,2,16,128]{3,2,1,0:T(8,128)S(1)}, f32[20,2,16,128]{3,2,1,0:T(8,128)S(1)}, u32[]{:S(2)}, u32[]{:S(2)}) collective-permute-start(f32[20,2,16,128]{3,2,1,0:T(8,128)S(1)} %get-tuple-element.172), channel_id=1, source_target_pairs={{0,4},{4,8},{8,12},{12,16},{16,20},{20,24},{24,28},{28,32},{32,36}... | collective-permute-start | bytes 983048 | tf_op jit(solution)/shard_map/ppermute | solution.py:43
  89.1 9.4 %collective-permute-start.11 = (f32[20,2,16,128]{3,2,1,0:T(8,128)S(1)}, f32[20,2,16,128]{3,2,1,0:T(8,128)S(1)}, u32[]{:S(2)}, u32[]{:S(2)}) collective-permute-start(f32[20,2,16,128]{3,2,1,0:T(8,128)S(1)} %get-tuple-element.173), channel_id=1, source_target_pairs={{4,0},{8,4},{12,8},{16,12},{20,16},{24,20},{28,24},{32,28},{36,32}... | collective-permute-start | bytes 983048 | tf_op jit(solution)/shard_map/ppermute | solution.py:45
  100.6 60.0 %copy-start.36 = (f32[8,4,128]{2,0,1:T(8,128)S(1)}, f32[8,4,128]{2,0,1:T(8,128)}, u32[]{:S(2)}) copy-start(f32[8,4,128]{2,0,1:T(8,128)} %get-tuple-element.80) | copy-start | bytes 49156
  102.5 65.6 %copy-start.3 = (f32[16,8,16,128]{3,2,1,0:T(8,128)}, f32[16,8,16,128]{3,2,1,0:T(8,128)S(1)}, u32[]{:S(2)}) copy-start(f32[16,8,16,128]{3,2,1,0:T(8,128)S(1)} %fusion.16) | copy-start | bytes 3145732
  102.5 58.8 %copy-start.35 = (f32[8,4,128]{2,0,1:T(8,128)S(1)}, f32[8,4,128]{2,0,1:T(8,128)}, u32[]{:S(2)}) copy-start(f32[8,4,128]{2,0,1:T(8,128)} %get-tuple-element.81) | copy-start | bytes 49156
  102.5 59.5 %copy-start.32 = (f32[8,4,128]{2,0,1:T(8,128)S(1)}, f32[8,4,128]{2,0,1:T(8,128)}, u32[]{:S(2)}) copy-start(f32[8,4,128]{2,0,1:T(8,128)} %copy-done.31) | copy-start | bytes 49156
  102.5 60.2 %copy-start.30 = (f32[8,4,128]{2,0,1:T(8,128)S(1)}, f32[8,4,128]{2,0,1:T(8,128)}, u32[]{:S(2)}) copy-start(f32[8,4,128]{2,0,1:T(8,128)} %copy-done.29) | copy-start | bytes 49156
  102.5 61.0 %copy-start.28 = (f32[8,4,128]{2,0,1:T(8,128)S(1)}, f32[8,4,128]{2,0,1:T(8,128)}, u32[]{:S(2)}) copy-start(f32[8,4,128]{2,0,1:T(8,128)} %copy-done.27) | copy-start | bytes 49156
  102.5 61.7 %copy-start.26 = (f32[8,4,128]{2,0,1:T(8,128)S(1)}, f32[8,4,128]{2,0,1:T(8,128)}, u32[]{:S(2)}) copy-start(f32[8,4,128]{2,0,1:T(8,128)} %copy-done.25) | copy-start | bytes 49156
  102.6 62.5 %copy-start.24 = (f32[8,4,128]{2,0,1:T(8,128)S(1)}, f32[8,4,128]{2,0,1:T(8,128)}, u32[]{:S(2)}) copy-start(f32[8,4,128]{2,0,1:T(8,128)} %copy-done.23) | copy-start | bytes 49156
  102.6 63.2 %copy-start.22 = (f32[8,4,128]{2,0,1:T(8,128)S(1)}, f32[8,4,128]{2,0,1:T(8,128)}, u32[]{:S(2)}) copy-start(f32[8,4,128]{2,0,1:T(8,128)} %copy-done.21) | copy-start | bytes 49156
  102.6 63.9 %copy-start.20 = (f32[8,4,128]{2,0,1:T(8,128)S(1)}, f32[8,4,128]{2,0,1:T(8,128)}, u32[]{:S(2)}) copy-start(f32[8,4,128]{2,0,1:T(8,128)} %copy-done.19) | copy-start | bytes 49156
  102.6 64.7 %copy-start.18 = (f32[8,4,128]{2,0,1:T(8,128)S(1)}, f32[8,4,128]{2,0,1:T(8,128)}, u32[]{:S(2)}) copy-start(f32[8,4,128]{2,0,1:T(8,128)} %copy-done.17) | copy-start | bytes 49156
  102.6 65.4 %copy-start.16 = (f32[8,4,128]{2,0,1:T(8,128)S(1)}, f32[8,4,128]{2,0,1:T(8,128)}, u32[]{:S(2)}) copy-start(f32[8,4,128]{2,0,1:T(8,128)} %copy-done.15) | copy-start | bytes 49156
  102.6 65.5 %copy-start.14 = (f32[8,4,128]{2,0,1:T(8,128)S(1)}, f32[8,4,128]{2,0,1:T(8,128)}, u32[]{:S(2)}) copy-start(f32[8,4,128]{2,0,1:T(8,128)} %copy-done.13) | copy-start | bytes 49156
  102.6 65.5 %copy-start.12 = (f32[8,4,128]{2,0,1:T(8,128)S(1)}, f32[8,4,128]{2,0,1:T(8,128)}, u32[]{:S(2)}) copy-start(f32[8,4,128]{2,0,1:T(8,128)} %copy-done.11) | copy-start | bytes 49156
  102.6 65.5 %copy-start.10 = (f32[8,4,128]{2,0,1:T(8,128)S(1)}, f32[8,4,128]{2,0,1:T(8,128)}, u32[]{:S(2)}) copy-start(f32[8,4,128]{2,0,1:T(8,128)} %copy-done.9) | copy-start | bytes 49156
  102.6 65.6 %copy-start.8 = (f32[8,4,128]{2,0,1:T(8,128)S(1)}, f32[8,4,128]{2,0,1:T(8,128)}, u32[]{:S(2)}) copy-start(f32[8,4,128]{2,0,1:T(8,128)} %copy-done.7) | copy-start | bytes 49156
  103.9 64.3 %copy-start.6 = (f32[8,4,128]{2,0,1:T(8,128)S(1)}, f32[8,4,128]{2,0,1:T(8,128)}, u32[]{:S(2)}) copy-start(f32[8,4,128]{2,0,1:T(8,128)} %copy-done.5) | copy-start | bytes 49156
  159.7 8.3 %copy-start.2 = (f32[8,4,128]{2,0,1:T(8,128)S(1)}, f32[8,4,128]{2,0,1:T(8,128)}, u32[]{:S(2)}) copy-start(f32[8,4,128]{2,0,1:T(8,128)} %reduce-scatter.2.cloned.1.call-done) | copy-start | bytes 49156
  168.4 4.4 %collective-permute-start.12 = (f32[20,1,4,128]{3,1,2,0:T(1,128)S(1)}, f32[20,1,4,128]{3,1,2,0:T(1,128)S(1)}, u32[]{:S(2)}, u32[]{:S(2)}) collective-permute-start(f32[20,1,4,128]{3,1,2,0:T(1,128)S(1)} %get-tuple-element.184), channel_id=1, source_target_pairs={{0,4},{4,8},{8,12},{12,16},{16,20},{20,24},{24,28},{28,32},{32,36}... | collective-permute-start | bytes 122888 | tf_op jit(solution)/shard_map/ppermute | solution.py:43
  171.5 4.7 %collective-permute-start.13 = (f32[20,1,4,128]{3,1,2,0:T(1,128)S(1)}, f32[20,1,4,128]{3,1,2,0:T(1,128)S(1)}, u32[]{:S(2)}, u32[]{:S(2)}) collective-permute-start(f32[20,1,4,128]{3,1,2,0:T(1,128)S(1)} %get-tuple-element.185), channel_id=1, source_target_pairs={{4,0},{8,4},{12,8},{16,12},{20,16},{24,20},{28,24},{32,28},{36,32}... | collective-permute-start | bytes 122888 | tf_op jit(solution)/shard_map/ppermute | solution.py:45
  176.3 7.0 %collective-permute-start.14 = (f32[20,10,1,128]{3,1,2,0:T(8,128)S(1)}, f32[20,10,1,128]{3,1,2,0:T(8,128)S(1)}, u32[]{:S(2)}, u32[]{:S(2)}) collective-permute-start(f32[20,10,1,128]{3,1,2,0:T(8,128)S(1)} %get-tuple-element.178), channel_id=1, source_target_pairs={{0,1},{1,2},{2,3},{4,5},{5,6},{6,7},{8,9},{9,10},{10,11},{12,13},{... | collective-permute-start | bytes 307208 | tf_op jit(solution)/shard_map/ppermute | solution.py:43
  181.0 8.1 %collective-permute-start.15 = (f32[20,10,1,128]{3,1,2,0:T(8,128)S(1)}, f32[20,10,1,128]{3,1,2,0:T(8,128)S(1)}, u32[]{:S(2)}, u32[]{:S(2)}) collective-permute-start(f32[20,10,1,128]{3,1,2,0:T(8,128)S(1)} %get-tuple-element.179), channel_id=1, source_target_pairs={{1,0},{2,1},{3,2},{5,4},{6,5},{7,6},{9,8},{10,9},{11,10},{13,12},{... | collective-permute-start | bytes 307208 | tf_op jit(solution)/shard_map/ppermute | solution.py:45
  (2 other events, 2.4 us)
Sparse Core Ops, SparseCore 0:
  104.7 54.9 reduce-scatter.1
where the time goes:
time: 203 us; the launch traced here: 199 us
  waiting for transfers between devices  89.1 us (44%)
  starting transfers between devices  48.5 us (24%)
  other arithmetic  34.2 us (17%)
  between operations  15.8 us (8%)
  blocking collectives  5.77 us (3%)
  local copies, waits for them, and re-layouts  4.62 us (2%)
    reduce_scatter x1, waiting for transfers between devices, local(): lax.psum_scatter(partial_value, 'tracer', scatter_dimension=1, tiled=True)  55.1 us
    ppermute x8, starting transfers between devices, padded_2(): lax.ppermute(tail, axis, [(i, (i + 1) % count) for i in range(ends)])  32.3 us
    ppermute x8, waiting for transfers between devices, padded_2(): lax.ppermute(head, axis, [((i + 1) % count, i) for i in range(ends)])  31.9 us
    ppermute x8, starting transfers between devices, padded_2(): lax.ppermute(head, axis, [((i + 1) % count, i) for i in range(ends)])  16.2 us
    add x6, other arithmetic, face_flux(): jnp.maximum(face_speed, 0.0) * left_state  13.3 us
    unnamed x57, other arithmetic  9.37 us
    all_gather x1, blocking collectives, local(): whole_flow = lax.all_gather(flow, 'tracer', axis=2, tiled=True)  5.77 us
  transfers between devices with their start and end apart: 17, of which 12 were waited for; matrix products, arithmetic and copies ran while one was open for 5% of the time, Pallas kernels for 0%

commit v1 on v0

v1 whole, which is shorter than its diff:
```python
import functools

import jax
import jax.numpy as jnp
from jax import lax
from jax.experimental import pallas as pl
from jax.experimental.pallas import tpu as pltpu
from jax.sharding import PartitionSpec as P

DIRS = (
    (0, 0, 0),
    (1, 0, 0),
    (-1, 0, 0),
    (0, 1, 0),
    (0, -1, 0),
    (0, 0, 1),
    (0, 0, -1),
    (1, 1, 0),
    (-1, -1, 0),
    (1, -1, 0),
    (-1, 1, 0),
    (1, 0, 1),
    (-1, 0, -1),
    (1, 0, -1),
    (-1, 0, 1),
    (0, 1, 1),
    (0, -1, -1),
    (0, 1, -1),
    (0, -1, 1),
)
WEIGHTS = (1.0 / 3.0,) + (1.0 / 18.0,) * 6 + (1.0 / 36.0,) * 12
OPP = (0, 2, 1, 4, 3, 6, 5, 8, 7, 10, 9, 12, 11, 14, 13, 16, 15, 18, 17)
RELAX = 1.25
XD = ((1, 7, 9, 11, 13), (2, 8, 10, 12, 14))
YD = ((3, 7, 10, 15, 17), (4, 8, 9, 16, 18))
CORNERS = ((7, -1, -1), (9, -1, 1), (10, 1, -1), (8, 1, 1))
CORNER_OF = {7: 0, 9: 1, 10: 2, 8: 3}
FLAG = 5
SX, NY, NZ = 8, 16, 128
TY = 4
CHUNKS = 4
F32 = jnp.float32


def kernel(
    n_space,
    n_tracer,
    decay_ref,
    coeff_ref,
    cells_ref,
    rates_ref,
    pop_hbm,
    mask_hbm,
    tracer_hbm,
    pop_out,
    vel_out,
    tracer_out,
    fin,
    mask_in,
    fluid_v,
    both,
    post,
    xs,
    xr,
    ys,
    yr,
    cs,
    cr,
    flow_f,
    fb,
    gflow,
    face_x,
    face_y,
    face_z,
    cext,
    csec,
    cout,
    emis,
    part,
    sb,
    rb,
    rx,
    fout,
    vout,
    load_sem,
    out_sem,
    halo_send,
    halo_recv,
    bulk_send,
    bulk_recv,
    flow_send,
    flow_recv,
    buoy_send,
    buoy_recv,
):
    sp = lax.axis_index("space")
    tr = lax.axis_index("tracer")
    space = {-1: lax.rem(sp + n_space - 1, n_space), 0: sp, 1: lax.rem(sp + 1, n_space)}
    trs = [lax.rem(tr + k, n_tracer) for k in range(n_tracer)]
    group = tracer_hbm.shape[0]
    piece = group // CHUNKS

    def rcopy(src, dst, ssem, rsem, ds, t):
        return pltpu.make_async_remote_copy(
            src_ref=src,
            dst_ref=dst,
            send_sem=ssem,
            recv_sem=rsem,
            device_id=(space[ds], t),
            device_id_type=pl.DeviceIdType.MESH,
        )

    load_pop = pltpu.make_async_copy(pop_hbm, fin, load_sem.at[0])
    load_mask = pltpu.make_async_copy(mask_hbm, mask_in, load_sem.at[1])
    load_tracer = pltpu.make_async_copy(tracer_hbm, cext.at[:, 4 : 4 + SX], load_sem.at[2])
    load_pop.start()
    load_mask.start()
    load_tracer.start()

    barrier = pltpu.get_barrier_semaphore()
    peers = [(ds, k) for ds in (-1, 0, 1) for k in range(n_tracer) if (ds, k) != (0, 0)]
    for ds, k in peers:
        pl.semaphore_signal(
            barrier, inc=1, device_id=(space[ds], trs[k]), device_id_type=pl.DeviceIdType.MESH
        )

    xi = lax.broadcasted_iota(jnp.int32, (SX, NZ), 0)
    zi = lax.broadcasted_iota(jnp.int32, (SX, NZ), 1)

    def moments(f):
        even = {}
        rho = f[0]
        u = [None, None, None]
        for q in range(1, 19, 2):
            rho = rho + (f[q] + f[q + 1])
            diff = f[q] - f[q + 1]
            for a in range(3):
                e = DIRS[q][a]
                if e == 1:
                    u[a] = diff if u[a] is None else u[a] + diff
                elif e == -1:
                    u[a] = -diff if u[a] is None else u[a] - diff
        inv = 1.0 / rho
        return rho, [v * inv for v in u]

    def collide(f, rho, u):
        base = 1.0 - 1.5 * (u[0] * u[0] + u[1] * u[1] + u[2] * u[2])
        scaled = RELAX * rho
        out = [None] * 19
        out[0] = (1.0 - RELAX) * f[0] + (WEIGHTS[0] * scaled) * base
        for q in range(1, 19, 2):
            along = None
            for a in range(3):
                e = DIRS[q][a]
                if e == 1:
                    along = u[a] if along is None else along + u[a]
                elif e == -1:
                    along = -u[a] if along is None else along - u[a]
            wr = WEIGHTS[q] * scaled
            sym = wr * (base + 4.5 * along * along)
            asym = wr * (3.0 * along)
            out[q] = (1.0 - RELAX) * f[q] + (sym + asym)
            out[q + 1] = (1.0 - RELAX) * f[q + 1] + (sym - asym)
        return out

    def keep_post(step, y, p):
        buf = step % 2
        for q in range(19):
            post[buf, q, y] = p[q]
        for k in range(5):
            xs[step, 0, k, y : y + 1, :] = p[XD[1][k]][0:1, :]
            xs[step, 1, k, y : y + 1, :] = p[XD[0][k]][SX - 1 : SX, :]
            if y == 0:
                ys[step, 0, k] = p[YD[1][k]]
            if y == TY - 1:
                ys[step, 1, k] = p[YD[0][k]]
        for c, (q, dx, dy) in enumerate(CORNERS):
            if y == (TY - 1 if dy < 0 else 0):
                row = p[q][SX - 1 : SX, :] if dx < 0 else p[q][0:1, :]
                cs[step, c, 0] = jnp.broadcast_to(row, (SX, NZ))

    def messages(step):
        n = 6 if step == 0 else 5
        part_of = pl.ds(0, n)
        m = 2 if step == 0 else 1
        out = []
        out.append((xs.at[step, 1, part_of], xr.at[step, 0, part_of], 1, 0))
        out.append((xs.at[step, 0, part_of], xr.at[step, 1, part_of], -1, 0))
        out.append((ys.at[step, 1, part_of], yr.at[step, 0, part_of], 0, 1))
        out.append((ys.at[step, 0, part_of], yr.at[step, 1, part_of], 0, n_tracer - 1))
        for c, (q, dx, dy) in enumerate(CORNERS):
            out.append(
                (
                    cs.at[step, c, pl.ds(0, m)],
                    cr.at[step, c, pl.ds(0, m)],
                    -dx,
                    1 if dy < 0 else n_tracer - 1,
                )
            )
        return [
            rcopy(s, d, halo_send.at[step, i], halo_recv.at[step, i], ds, trs[k])
            for i, (s, d, ds, k) in enumerate(out)
        ]

    def bulk(j):
        rows = pl.ds(j * piece, piece)
        return (
            rcopy(
                tracer_hbm.at[rows, pl.ds(SX - 4, 4)],
                cext.at[rows, pl.ds(0, 4)],
                bulk_send.at[0, j],
                bulk_recv.at[0, j],
                1,
                tr,
            ),
            rcopy(
                tracer_hbm.at[rows, pl.ds(0, 4)],
                cext.at[rows, pl.ds(SX + 4, 4)],
                bulk_send.at[1, j],
                bulk_recv.at[1, j],
                -1,
                tr,
            ),
        )

    def shifted(step, buf, q, y):
        ex, ey, ez = DIRS[q]
        yy = y - ey
        if yy < 0:
            v = yr[step, 0, YD[0].index(q)]
        elif yy >= TY:
            v = yr[step, 1, YD[1].index(q)]
        else:
            v = post[buf, q, yy]
        if ex != 0:
            side = 0 if ex == 1 else 1
            if 0 <= yy < TY:
                row = xr[step, side, XD[side].index(q), yy : yy + 1, :]
            else:
                row = cr[step, CORNER_OF[q], 0, 0:1, :]
            v = pltpu.roll(v, 1 if ex == 1 else SX - 1, 0)
            v = jnp.where(xi == (0 if ex == 1 else SX - 1), row, v)
        if ez != 0:
            v = pltpu.roll(v, 1 if ez == 1 else NZ - 1, 1)
        return v

    def stream(step, y):
        buf = step % 2
        air = fluid_v[y] > 0.5
        here = [post[buf, q, y] for q in range(19)]
        fresh = [here[0]]
        for q in range(1, 19):
            back = jnp.where(air, here[OPP[q]], here[q])
            fresh.append(jnp.where(both[q, y] > 0.5, shifted(step, buf, q, y), back))
        return fresh

    load_mask.wait()
    for y in range(TY):
        m = mask_in[pl.ds(y, SX, stride=TY), :]
        air = 1.0 - m.astype(F32)
        fluid_v[y] = air
        for side, x in ((0, 0), (1, SX - 1)):
            xs[0, side, FLAG, y : y + 1, :] = air[x : x + 1, :]
        if y == 0:
            ys[0, 0, FLAG] = air
        if y == TY - 1:
            ys[0, 1, FLAG] = air
        for c, (q, dx, dy) in enumerate(CORNERS):
            if y == (TY - 1 if dy < 0 else 0):
                row = air[SX - 1 : SX, :] if dx < 0 else air[0:1, :]
                cs[0, c, 1] = jnp.broadcast_to(row, (SX, NZ))
    load_pop.wait()
    for y in range(TY):
        f = [fin[pl.ds(q * SX * TY + y, SX, stride=TY), :] for q in range(19)]
        rho, u = moments(f)
        keep_post(0, y, collide(f, rho, u))

    pl.semaphore_wait(barrier, len(peers))
    first = messages(0)
    for c in first:
        c.start()
    sent_bulk = [bulk(j) for j in range(CHUNKS)]
    for c in sent_bulk[0]:
        c.start()

    yi16 = lax.broadcasted_iota(jnp.int32, (NY, NZ), 0)
    zi16 = lax.broadcasted_iota(jnp.int32, (NY, NZ), 1)
    flat = yi16 * NZ + zi16
    origin = (sp * SX - 2) * (NY * NZ)

    def emit(t, carry):
        for r in range(SX + 4):
            total = jnp.zeros((NY, NZ), F32)
            for s in range(cells_ref.shape[0]):
                key = cells_ref[s, t] - (origin + r * NY * NZ)
                total = total + jnp.where(flat == key, rates_ref[s, t], 0.0)
            emis[t, r] = total
        return carry

    lax.fori_loop(0, group, emit, 0)

    for c in first:
        c.wait_recv()

    has_x = (
        jnp.where(sp > 0, 1.0, 0.0).astype(F32),
        jnp.where(sp < n_space - 1, 1.0, 0.0).astype(F32),
    )
    has_y = (
        jnp.where(tr > 0, 1.0, 0.0).astype(F32),
        jnp.where(tr < n_tracer - 1, 1.0, 0.0).astype(F32),
    )
    for y in range(TY):
        mine = fluid_v[y]
        for q in range(1, 19):
            ex, ey, ez = DIRS[q]
            yy = y - ey
            if yy < 0:
                v = yr[0, 0, FLAG] * has_y[0]
            elif yy >= TY:
                v = yr[0, 1, FLAG] * has_y[1]
            else:
                v = fluid_v[yy]
            if ex != 0:
                side = 0 if ex == 1 else 1
                if 0 <= yy < TY:
                    row = xr[0, side, FLAG, yy : yy + 1, :] * has_x[side]
                else:
                    row = cr[0, CORNER_OF[q], 1, 0:1, :] * (has_x[side] * has_y[0 if yy < 0 else 1])
                v = pltpu.roll(v, 1 if ex == 1 else SX - 1, 0)
                v = jnp.where(xi == (0 if ex == 1 else SX - 1), row, v)
            if ez != 0:
                v = pltpu.roll(v, 1 if ez == 1 else NZ - 1, 1)
                v = jnp.where(zi == (0 if ez == 1 else NZ - 1), 0.0, v)
            both[q, y] = v * mine

    for y in range(TY):
        f = stream(0, y)
        rho, u = moments(f)
        keep_post(1, y, collide(f, rho, u))
    second = messages(1)
    for c in second:
        c.start()
    for c in sent_bulk[1]:
        c.start()
    for c in second:
        c.wait_recv()

    for y in range(TY):
        f = stream(1, y)
        rho, u = moments(f)
        air = fluid_v[y]
        for a in range(3):
            flow_f[pl.ds(a * TY + y, SX, stride=4 * TY), :] = u[a] * air
        flow_f[pl.ds(3 * TY + y, SX, stride=4 * TY), :] = air
        keep_post(2, y, collide(f, rho, u))
    for x in range(SX):
        fb[tr, 3 + x] = flow_f[x * 4 * TY : (x + 1) * 4 * TY, :].astype(jnp.bfloat16)

    def flow_messages():
        out = []
        for ds in (0, 1, -1):
            for k in range(n_tracer):
                if (ds, k) == (0, 0):
                    continue
                if ds == 0:
                    src, dst, kind = pl.ds(3, SX), pl.ds(3, SX), 0
                elif ds == 1:
                    src, dst, kind = pl.ds(SX, 3), pl.ds(0, 3), 1
                else:
                    src, dst, kind = pl.ds(3, 3), pl.ds(SX + 3, 3), 2
                out.append(
                    rcopy(
                        fb.at[tr, src],
                        fb.at[tr, dst],
                        flow_send.at[kind, k],
                        flow_recv.at[kind, tr],
                        ds,
                        trs[k],
                    )
                )
        return out

    def flow_arrivals():
        out = []
        for kind, rows in ((0, pl.ds(3, SX)), (1, pl.ds(0, 3)), (2, pl.ds(SX + 3, 3))):
            for k in range(n_tracer):
                if (kind, k) == (0, 0):
                    continue
                t = trs[k]
                out.append(
                    rcopy(
                        fb.at[t, rows],
                        fb.at[t, rows],
                        flow_send.at[kind, k],
                        flow_recv.at[kind, t],
                        1,
                        t,
                    )
                )
        return out

    flows = flow_messages()
    for c in flows:
        c.start()
    third = messages(2)
    for c in third:
        c.start()
    for j in range(2, CHUNKS):
        for c in sent_bulk[j]:
            c.start()
    load_tracer.wait()
    for c in flow_arrivals():
        c.wait_recv()

    def widen(x, carry):
        for t in range(n_tracer):
            v = fb[t, x].astype(F32)
            for a in range(4):
                gflow[a, x, t * TY : (t + 1) * TY, :] = v[a * TY : (a + 1) * TY, :]
        return carry

    lax.fori_loop(0, SX + 6, widen, 0)

    @pl.when(sp == 0)
    def _():
        for x in range(3):
            gflow[3, x] = jnp.zeros((NY, NZ), F32)

    @pl.when(sp == n_space - 1)
    def _():
        for x in range(SX + 3, SX + 6):
            gflow[3, x] = jnp.zeros((NY, NZ), F32)

    def split(ref, i, s):
        ref[0, i] = jnp.maximum(s, 0.0)
        ref[1, i] = jnp.minimum(s, 0.0)

    def faces_x(i, carry):
        split(
            face_x,
            i,
            0.5 * (gflow[0, i] + gflow[0, i + 1]) * gflow[3, i] * gflow[3, i + 1],
        )
        return carry

    lax.fori_loop(0, SX + 5, faces_x, 0)

    def faces_yz(i, carry):
        air = gflow[3, i + 1]
        v = gflow[1, i + 1]
        s = 0.5 * (v + pltpu.roll(v, NY - 1, 0)) * air * pltpu.roll(air, NY - 1, 0)
        split(face_y, i, jnp.where(yi16 == NY - 1, 0.0, s))
        v = gflow[2, i + 1]
        s = 0.5 * (v + pltpu.roll(v, NZ - 1, 1)) * air * pltpu.roll(air, NZ - 1, 1)
        split(face_z, i, jnp.where(zi16 == NZ - 1, 0.0, s))
        return carry

    lax.fori_loop(0, SX + 4, faces_yz, 0)

    def limited(below, above):
        return 0.5 * jnp.minimum(
            jnp.maximum(below, jnp.minimum(above, 0.0)), jnp.maximum(above, 0.0)
        )

    def along_axis(c, axis, size, index, up, down):
        above = jnp.where(index == size - 1, 0.0, pltpu.roll(c, size - 1, axis)) - c
        below = c - jnp.where(index == 0, 0.0, pltpu.roll(c, 1, axis))
        h = limited(below, above)
        flux = up * (c + h) + down * pltpu.roll(c - h, size - 1, axis)
        return flux - pltpu.roll(flux, 1, axis)

    def section(src, t, rows, face_shift, yz_shift, emit_shift, store):
        rate = decay_ref[t]
        before = jnp.maximum(t - 1, 0)
        gain = jnp.where(lax.rem(t, 2) == 1, decay_ref[before], 0.0)
        below = src[t, 1] - src[t, 0]
        flux_low = None
        left_low = None
        for j in range(1, rows + 3):
            c = src[t, j]
            above = src[t, j + 1] - c
            h = limited(below, above)
            if j >= 2:
                f = j - 1 + face_shift
                flux = face_x[0, f] * left_low + face_x[1, f] * (c - h)
                if j >= 3:
                    r = j - 3
                    mid = src[t, j - 1]
                    div = flux - flux_low
                    i = r + yz_shift
                    div = div + along_axis(mid, 0, NY, yi16, face_y[0, i], face_y[1, i])
                    div = div + along_axis(mid, 1, NZ, zi16, face_z[0, i], face_z[1, i])
                    made = gain * src[before, j - 1] - rate * mid
                    store(r, mid + (made - div + emis[t, r + emit_shift]))
                flux_low = flux
            left_low = c + h
            below = above

    def section_one(j, carry):
        for c in bulk(j):
            c.wait_recv()

        def clear(rows):
            def body(t, carry):
                for x in rows:
                    cext[j * piece + t, x] = jnp.zeros((NY, NZ), F32)
                return carry

            lax.fori_loop(0, piece, body, 0)

        @pl.when(sp == 0)
        def _():
            clear(range(4))

        @pl.when(sp == n_space - 1)
        def _():
            clear(range(SX + 4, SX + 8))

        def one(i, carry):
            t = j * piece + i

            def store(r, v):
                csec[t, r] = v

            section(cext, t, SX + 4, -1, 0, 0, store)
            return carry

        return lax.fori_loop(0, piece, one, carry)

    lax.fori_loop(0, CHUNKS, section_one, 0)

    for x in range(SX):
        part[x] = jnp.zeros((NY, NZ), F32)

    def section_two(t, carry):
        weight = coeff_ref[t]

        def store(r, v):
            cout[t, r] = v
            part[r] = part[r] + weight * v

        section(csec, t, SX, 1, 2, 2, store)
        return carry

    lax.fori_loop(0, group, section_two, 0)
    save_tracer = pltpu.make_async_copy(cout, tracer_out, out_sem.at[0])
    save_tracer.start()

    for x in range(SX):
        v = part[x]
        for t in range(n_tracer):
            sb[t, x * 8 : (x + 1) * 8, :] = pltpu.roll(v, (1 - TY * t) % NY, 0)[0:8]
    buoy = []
    for ds, rows, dst in ((1, pl.ds((SX - 1) * 8, 8), 0), (-1, pl.ds(0, 8), 1)):
        for k in range(n_tracer):
            buoy.append(
                rcopy(
                    sb.at[trs[k], rows],
                    rx.at[dst, k],
                    buoy_send.at[dst + 1, k],
                    buoy_recv.at[dst + 1, k],
                    ds,
                    trs[k],
                )
            )
    for k in range(1, n_tracer):
        buoy.append(
            rcopy(sb.at[trs[k]], rb.at[k], buoy_send.at[0, k], buoy_recv.at[0, k], 0, trs[k])
        )
    for c in buoy:
        c.start()
    for c in third:
        c.wait_recv()
    for c in buoy:
        c.wait_recv()

    buf = 0
    for yy in range(-1, TY + 1):
        g = sb[tr, pl.ds(yy + 1, SX, stride=8), :]
        for k in range(1, n_tracer):
            g = g + rb[k, pl.ds(yy + 1, SX, stride=8), :]
        if yy < 0 or yy >= TY:
            side = 0 if yy < 0 else 1
            for k, q in enumerate(YD[side]):
                if DIRS[q][2]:
                    yr[2, side, k] = yr[2, side, k] + (3.0 * WEIGHTS[q] * DIRS[q][2]) * g
        else:
            for q in range(19):
                if DIRS[q][2]:
                    post[buf, q, yy] = post[buf, q, yy] + (3.0 * WEIGHTS[q] * DIRS[q][2]) * g
    for side in range(2):
        g = rx[side, 0]
        for k in range(1, n_tracer):
            g = g + rx[side, k]
        g = pltpu.roll(g, 7, 0)
        for k, q in enumerate(XD[side]):
            if DIRS[q][2]:
                xr[2, side, k] = xr[2, side, k] + (3.0 * WEIGHTS[q] * DIRS[q][2]) * g

    for y in range(TY):
        f = stream(2, y)
        rho, u = moments(f)
        for q in range(19):
            fout[pl.ds(q * SX * TY + y, SX, stride=TY), :] = f[q]
        for a in range(3):
            vout[pl.ds(a * SX * TY + y, SX, stride=TY), :] = u[a] * fluid_v[y]
    save_pop = pltpu.make_async_copy(fout, pop_out, out_sem.at[1])
    save_vel = pltpu.make_async_copy(vout, vel_out, out_sem.at[2])
    save_pop.start()
    save_vel.start()

    for c in first + second + third + flows + buoy:
        c.wait_send()
    for pair in sent_bulk:
        for c in pair:
            c.wait_send()
    save_tracer.wait()
    save_pop.wait()
    save_vel.wait()


def local(
    n_space,
    n_tracer,
    populations,
    solid_mask,
    tracers,
    decay_rates,
    buoyancy_coeffs,
    source_cells,
    source_rates,
):
    group = tracers.shape[0]
    rows = SX * TY
    smem = pl.BlockSpec(memory_space=pltpu.SMEM)
    hbm = pl.BlockSpec(memory_space=pl.ANY)
    vmem = pltpu.VMEM
    dma = pltpu.SemaphoreType.DMA
    out = pl.pallas_call(
        functools.partial(kernel, n_space, n_tracer),
        out_shape=(
            jax.ShapeDtypeStruct((19 * rows, NZ), F32),
            jax.ShapeDtypeStruct((3 * rows, NZ), F32),
            jax.ShapeDtypeStruct(tracers.shape, F32),
        ),
        in_specs=[smem] * 4 + [hbm] * 3,
        out_specs=(hbm, hbm, hbm),
        scratch_shapes=[
            vmem((19 * rows, NZ), F32),
            vmem((rows, NZ), jnp.int32),
            vmem((TY, SX, NZ), F32),
            vmem((19, TY, SX, NZ), F32),
            vmem((2, 19, TY, SX, NZ), F32),
            vmem((3, 2, 6, 8, NZ), F32),
            vmem((3, 2, 6, 8, NZ), F32),
            vmem((3, 2, 6, 8, NZ), F32),
            vmem((3, 2, 6, 8, NZ), F32),
            vmem((3, 4, 2, 8, NZ), F32),
            vmem((3, 4, 2, 8, NZ), F32),
            vmem((SX * 4 * TY, NZ), F32),
            vmem((n_tracer, SX + 6, 4 * TY, NZ), jnp.bfloat16),
            vmem((4, SX + 6, NY, NZ), F32),
            vmem((2, SX + 5, NY, NZ), F32),
            vmem((2, SX + 4, NY, NZ), F32),
            vmem((2, SX + 4, NY, NZ), F32),
            vmem((group, SX + 8, NY, NZ), F32),
            vmem((group, SX + 4, NY, NZ), F32),
            vmem((group, SX, NY, NZ), F32),
            vmem((group, SX + 4, NY, NZ), F32),
            vmem((SX, NY, NZ), F32),
            vmem((n_tracer, SX * 8, NZ), F32),
            vmem((n_tracer, SX * 8, NZ), F32),
            vmem((2, n_tracer, 8, NZ), F32),
            vmem((19 * rows, NZ), F32),
            vmem((3 * rows, NZ), F32),
            dma((3,)),
            dma((3,)),
            dma((3, 8)),
            dma((3, 8)),
            dma((2, CHUNKS)),
            dma((2, CHUNKS)),
            dma((3, n_tracer)),
            dma((3, n_tracer)),
            dma((3, n_tracer)),
            dma((3, n_tracer)),
        ],
        compiler_params=pltpu.CompilerParams(
            collective_id=0, has_side_effects=True, vmem_limit_bytes=40 * 1024 * 1024
        ),
        name="plume",
    )(
        decay_rates,
        buoyancy_coeffs,
        source_cells.T,
        source_rates.T,
        populations.reshape(19 * rows, NZ),
        solid_mask.reshape(rows, NZ),
        tracers,
    )
    return (
        out[0].reshape(populations.shape),
        out[1].reshape((3,) + populations.shape[1:]),
        out[2],
    )


def solution(mesh):
    placed = (
        P(None, "space", "tracer", None),
        P("space", "tracer", None),
        P("tracer", "space", None, None),
        P("tracer"),
        P("tracer"),
        P("tracer", None),
        P("tracer", None),
    )
    return jax.shard_map(
        functools.partial(local, mesh.shape["space"], mesh.shape["tracer"]),
        mesh=mesh,
        in_specs=placed,
        out_specs=(
            P(None, "space", "tracer", None),
            P(None, "space", "tracer", None),
            P("tracer", "space", None, None),
        ),
        check_vma=False,
    )
```

time: 203 us -> 66.1 us (0.33); the launches traced: 199 us -> 65.8 us
  waiting for transfers between devices: 89.1 us -> 0 us
  Pallas kernels: 0 us -> 58.6 us
  starting transfers between devices: 48.5 us -> 0 us
  other arithmetic: 34.2 us -> 0 us
  between operations: 15.8 us -> 0.67 us
  blocking collectives: 5.77 us -> 0 us
    pallas_call x0 -> x1, Pallas kernels: none -> 58.6 us  [local(): pl.pallas_call(functools.partial(kernel, n_space, n_tracer), out_shape=(j...]
    reduce_scatter x1 -> x0, waiting for transfers between devices: 55.1 us -> none  [local(): lax.psum_scatter(partial_value, 'tracer', scatter_dimension=1, tiled=True)]
    ppermute x16 -> x0, starting transfers between devices: 48.4 us -> none  [the longest x8 32.3 us: padded_2(): lax.ppermute(tail, axis, [(i, (i + 1) % count) for i in range(ends)])]
    ppermute x16 -> x0, waiting for transfers between devices: 34 us -> none  [the longest x8 31.9 us: padded_2(): lax.ppermute(head, axis, [((i + 1) % count, i) for i in range(ends)])]
    add x8 -> x0, other arithmetic: 15.3 us -> none  [the longest x6 13.3 us: face_flux(): jnp.maximum(face_speed, 0.0) * left_state]
    unnamed x57 -> x0, other arithmetic: 9.37 us -> none
    all_gather x1 -> x0, blocking collectives: 5.77 us -> none  [local(): whole_flow = lax.all_gather(flow, 'tracer', axis=2, tiled=True)]
    unnamed x117 -> x17, local copies, waits for them, and re-layouts: 2.2 us -> 6.57 us
  transfers between devices with their start and end apart: 17 -> 0, of which waited for: 12 -> 0; matrix products, arithmetic and copies ran while one was open for 5% -> 0% of each run, Pallas kernels for 0% -> 0%
where the time goes in v1:
time: 66.1 us; the launch traced here: 65.8 us
  Pallas kernels  58.6 us (89%)
  local copies, waits for them, and re-layouts  6.57 us (10%)
  between operations  0.67 us (1%)
    pallas_call x1, Pallas kernels, local(): pl.pallas_call(functools.partial(kernel, n_space, n_tracer), out_shape=(j...  58.6 us
    unnamed x17, local copies, waits for them, and re-layouts  6.57 us

profile of v1, /device:TPU:1, one launch (start us, length us, event | category | flops | bytes accessed | tf_op | source)
XLA Modules:
  0.0 65.8 jit_solution(15877892426985962861)
XLA Ops:
  0.6 0.0 copy-start.3
  0.6 0.0 copy-start.5
  0.7 0.0 copy-start.6
  0.7 0.7 copy-done.3
  1.3 0.0 copy-done.5
  1.3 0.0 copy-done.6
  1.3 0.0 copy-start
  1.3 1.2 %copy-done = f32[16,8,16,128]{3,2,1,0:T(8,128)S(1)} copy-done((f32[16,8,16,128]{3,2,1,0:T(8,128)S(1)}, f32[16,8,16,128]{3,2,1,0:T(8,128)}, u32[]{:S(2)}) %copy-start) | copy-done | bytes 1048600
  2.6 0.0 copy-start.1
  2.6 1.0 %copy-done.1 = f32[19,8,4,128]{3,2,1,0:T(4,128)S(1)} copy-done((f32[19,8,4,128]{3,2,1,0:T(4,128)S(1)}, f32[19,8,4,128]{3,2,1,0:T(4,128)}, u32[]{:S(2)}) %copy-start.1) | copy-done | bytes 311320
  3.5 0.0 copy-start.2
  3.5 0.7 %copy-done.2 = s32[8,4,128]{2,1,0:T(4,128)S(1)} copy-done((s32[8,4,128]{2,1,0:T(4,128)S(1)}, s32[8,4,128]{2,1,0:T(4,128)}, u32[]{:S(2)}) %copy-start.2) | copy-done | bytes 16408
  4.2 0.0 copy-start.4
  4.2 0.7 %copy-done.4 = f32[16,8]{0,1:T(8,128)S(1)} copy-done((f32[16,8]{0,1:T(8,128)S(1)}, f32[16,8]{0,1:T(8,128)}, u32[]{:S(2)}) %copy-start.4) | copy-done | bytes 536
  4.9 58.6 %plume.1 = (f32[608,128]{1,0:T(8,128)S(1)}, f32[96,128]{1,0:T(8,128)S(1)}, f32[16,8,16,128]{3,2,1,0:T(8,128)S(1)}) custom-call(f32[16]{0:T(128)S(1)} %copy-done.5, f32[16]{0:T(128)S(1)} %copy-done.6, s32[8,16]{1,0:T(8,128)S(1)} %bitcast.10, f32[8,16]{1,0:T(8,128)S(1)} %bitcast.11, f32[608,128]{1,0:T(8,128)S(1)} %bitcast.6, s32[32,128]{1,0:T(8,128)S(1)} %bitcast.9, ...), custom_call_target="tpu_custom_call" | custom-call | tf_op jit(solution)/shard_map/plume/pallas_call | solution.py:640
  63.5 0.7 %copy.13 = f32[19,8,4,128]{3,2,1,0:T(4,128)} copy(f32[19,8,4,128]{3,2,1,0:T(4,128)S(1)} %bitcast.7) | data formatting | bytes 622592
  64.2 0.6 copy.14
  64.8 1.0 %copy.15 = f32[16,8,16,128]{3,2,1,0:T(8,128)} copy(f32[16,8,16,128]{3,2,1,0:T(8,128)S(1)} %get-tuple-element.14) | data formatting | bytes 2097152
Async XLA Ops:
  0.6 0.7 %copy-start.3 = (s32[16,8]{0,1:T(8,128)S(1)}, s32[16,8]{0,1:T(8,128)}, u32[]{:S(2)}) copy-start(s32[16,8]{0,1:T(8,128)} %param.12) | copy-start | bytes 1540
  0.6 0.7 %copy-start.5 = (f32[16]{0:T(128)S(1)}, f32[16]{0:T(128)}, u32[]{:S(2)}) copy-start(f32[16]{0:T(128)} %decay_ref.1) | copy-start | bytes 196
  0.7 0.7 %copy-start.6 = (f32[16]{0:T(128)S(1)}, f32[16]{0:T(128)}, u32[]{:S(2)}) copy-start(f32[16]{0:T(128)} %coeff_ref.1) | copy-start | bytes 196
  1.3 1.2 %copy-start = (f32[16,8,16,128]{3,2,1,0:T(8,128)S(1)}, f32[16,8,16,128]{3,2,1,0:T(8,128)}, u32[]{:S(2)}) copy-start(f32[16,8,16,128]{3,2,1,0:T(8,128)} %tracer_hbm.1) | copy-start | bytes 3145732
  2.6 1.0 %copy-start.1 = (f32[19,8,4,128]{3,2,1,0:T(4,128)S(1)}, f32[19,8,4,128]{3,2,1,0:T(4,128)}, u32[]{:S(2)}) copy-start(f32[19,8,4,128]{3,2,1,0:T(4,128)} %param.7) | copy-start | bytes 933892
  3.5 0.7 %copy-start.2 = (s32[8,4,128]{2,1,0:T(4,128)S(1)}, s32[8,4,128]{2,1,0:T(4,128)}, u32[]{:S(2)}) copy-start(s32[8,4,128]{2,1,0:T(4,128)} %param.8) | copy-start | bytes 49156
  4.2 0.7 %copy-start.4 = (f32[16,8]{0,1:T(8,128)S(1)}, f32[16,8]{0,1:T(8,128)}, u32[]{:S(2)}) copy-start(f32[16,8]{0,1:T(8,128)} %param.13) | copy-start | bytes 1540

commit v2 on v1

--- a/solution.py
+++ b/solution.py
@@ -38,23 +38,28 @@
 FLAG = 5
 SX, NY, NZ = 8, 16, 128
 TY = 4
-CHUNKS = 4
+CHUNKS = 8
+FIRST, SECOND = 3, 6
 F32 = jnp.float32
 
 
 def kernel(
     n_space,
     n_tracer,
-    decay_ref,
-    coeff_ref,
-    cells_ref,
-    rates_ref,
+    decay_hbm,
+    coeff_hbm,
+    cells_hbm,
+    rates_hbm,
     pop_hbm,
     mask_hbm,
     tracer_hbm,
     pop_out,
     vel_out,
     tracer_out,
+    decay_ref,
+    coeff_ref,
+    cells_ref,
+    rates_ref,
     fin,
     mask_in,
     fluid_v,
@@ -73,6 +78,15 @@
     face_y,
     face_z,
     cext,
+    outer_s,
+    outer_r,
+    lx,
+    hx,
+    ly,
+    hy,
+    lz,
+    hz,
+    base,
     csec,
     cout,
     emis,
@@ -113,16 +127,97 @@
     load_pop = pltpu.make_async_copy(pop_hbm, fin, load_sem.at[0])
     load_mask = pltpu.make_async_copy(mask_hbm, mask_in, load_sem.at[1])
     load_tracer = pltpu.make_async_copy(tracer_hbm, cext.at[:, 4 : 4 + SX], load_sem.at[2])
+    scalars = [
+        pltpu.make_async_copy(a, b, load_sem.at[3 + i])
+        for i, (a, b) in enumerate(
+            (
+                (cells_hbm, cells_ref),
+                (rates_hbm, rates_ref),
+                (decay_hbm, decay_ref),
+                (coeff_hbm, coeff_ref),
+            )
+        )
+    ]
+
+    along_x = {-1: sp > 0, 1: sp < n_space - 1}
+    along_y = {-1: tr > 0, 1: tr < n_tracer - 1}
+
+    def where_there(ds, dt, body):
+        if ds != 0 and dt != 0:
+            pl.when(jnp.logical_and(along_x[ds], along_y[dt]))(body)
+        elif ds != 0:
+            pl.when(along_x[ds])(body)
+        elif dt != 0:
+            pl.when(along_y[dt])(body)
+        else:
+            body()
+
+    barrier = pltpu.get_barrier_semaphore()
+
+    def greet(ds):
+        def body():
+            for k in range(n_tracer):
+                if (ds, k) != (0, 0):
+                    pl.semaphore_signal(
+                        barrier,
+                        inc=1,
+                        device_id=(space[ds], trs[k]),
+                        device_id_type=pl.DeviceIdType.MESH,
+                    )
+
+        where_there(ds, 0, body)
+
+    for ds in (-1, 1, 0):
+        greet(ds)
     load_pop.start()
     load_mask.start()
     load_tracer.start()
-
-    barrier = pltpu.get_barrier_semaphore()
-    peers = [(ds, k) for ds in (-1, 0, 1) for k in range(n_tracer) if (ds, k) != (0, 0)]
-    for ds, k in peers:
-        pl.semaphore_signal(
-            barrier, inc=1, device_id=(space[ds], trs[k]), device_id_type=pl.DeviceIdType.MESH
-        )
+    for c in scalars:
+        c.start()
+
+    def clear_x(ds):
+        side = 0 if ds < 0 else 1
+
+        @pl.when(jnp.logical_not(along_x[ds]))
+        def _():
+            xr[0, side, FLAG] = jnp.zeros((8, NZ), F32)
+            for step in range(3):
+                for k in range(5):
+                    xr[step, side, k] = jnp.zeros((8, NZ), F32)
+                for c in range(4):
+                    if CORNERS[c][1] == ds:
+                        for m in range(2):
+                            cr[step, c, m] = jnp.zeros((8, NZ), F32)
+            for t in range(n_tracer):
+                for x in range(3):
+                    fb[t, x if ds < 0 else SX + 3 + x] = jnp.zeros((4 * TY, NZ), jnp.bfloat16)
+                rx[side, t] = jnp.zeros((8, NZ), F32)
+
+            def body(t, carry):
+                for x in range(2):
+                    cext[t, (2 if ds < 0 else SX + 4) + x] = jnp.zeros((NY, NZ), F32)
+                    outer_r[side, t, x] = jnp.zeros((NY, NZ), jnp.bfloat16)
+                return carry
+
+            lax.fori_loop(0, group, body, 0)
+
+    def clear_y(dt):
+        side = 0 if dt < 0 else 1
+
+        @pl.when(jnp.logical_not(along_y[dt]))
+        def _():
+            yr[0, side, FLAG] = jnp.zeros((8, NZ), F32)
+            for step in range(3):
+                for k in range(5):
+                    yr[step, side, k] = jnp.zeros((8, NZ), F32)
+                for c in range(4):
+                    if CORNERS[c][2] == dt:
+                        for m in range(2):
+                            cr[step, c, m] = jnp.zeros((8, NZ), F32)
+
+    for d in (-1, 1):
+        clear_x(d)
+        clear_y(d)
 
     xi = lax.broadcasted_iota(jnp.int32, (SX, NZ), 0)
     zi = lax.broadcasted_iota(jnp.int32, (SX, NZ), 1)
@@ -180,48 +275,88 @@
                 cs[step, c, 0] = jnp.broadcast_to(row, (SX, NZ))
 
     def messages(step):
-        n = 6 if step == 0 else 5
-        part_of = pl.ds(0, n)
-        m = 2 if step == 0 else 1
+        part_of = pl.ds(0, 6 if step == 0 else 5)
+        m = pl.ds(0, 2 if step == 0 else 1)
+        out = [
+            (xs.at[step, 1, part_of], xr.at[step, 0, part_of], 1, 0),
+            (xs.at[step, 0, part_of], xr.at[step, 1, part_of], -1, 0),
+        ]
+        for c, (q, dx, dy) in enumerate(CORNERS):
+            out.append((cs.at[step, c, m], cr.at[step, c, m], -dx, -dy))
+        out.append((ys.at[step, 1, part_of], yr.at[step, 0, part_of], 0, 1))
+        out.append((ys.at[step, 0, part_of], yr.at[step, 1, part_of], 0, -1))
+        return [
+            (
+                rcopy(
+                    s,
+                    d,
+                    halo_send.at[step, i],
+                    halo_recv.at[step, i],
+                    ds,
+                    trs[dt % n_tracer],
+                ),
+                ds,
+                dt,
+            )
+            for i, (s, d, ds, dt) in enumerate(out)
+        ]
+
+    def start(copies):
+        for c, ds, dt in copies:
+            where_there(ds, dt, c.start)
+
+    def arrive(copies):
+        for c, ds, dt in copies:
+            where_there(-ds, -dt, c.wait_recv)
+
+    def leave(copies):
+        for c, ds, dt in copies:
+            where_there(ds, dt, c.wait_send)
+
+    def bulk(j):
+        rows = pl.ds(j * piece, piece)
         out = []
-        out.append((xs.at[step, 1, part_of], xr.at[step, 0, part_of], 1, 0))
-        out.append((xs.at[step, 0, part_of], xr.at[step, 1, part_of], -1, 0))
-        out.append((ys.at[step, 1, part_of], yr.at[step, 0, part_of], 0, 1))
-        out.append((ys.at[step, 0, part_of], yr.at[step, 1, part_of], 0, n_tracer - 1))
-        for c, (q, dx, dy) in enumerate(CORNERS):
+        for i, (ds, near, there, far) in enumerate(((1, SX - 2, 2, 0), (-1, 0, SX + 4, 1))):
             out.append(
                 (
-                    cs.at[step, c, pl.ds(0, m)],
-                    cr.at[step, c, pl.ds(0, m)],
-                    -dx,
-                    1 if dy < 0 else n_tracer - 1,
+                    rcopy(
+                        tracer_hbm.at[rows, pl.ds(near, 2)],
+                        cext.at[rows, pl.ds(there, 2)],
+                        bulk_send.at[i, j],
+                        bulk_recv.at[i, j],
+                        ds,
+                        tr,
+                    ),
+                    ds,
+                    0,
                 )
             )
-        return [
-            rcopy(s, d, halo_send.at[step, i], halo_recv.at[step, i], ds, trs[k])
-            for i, (s, d, ds, k) in enumerate(out)
-        ]
-
-    def bulk(j):
-        rows = pl.ds(j * piece, piece)
-        return (
-            rcopy(
-                tracer_hbm.at[rows, pl.ds(SX - 4, 4)],
-                cext.at[rows, pl.ds(0, 4)],
-                bulk_send.at[0, j],
-                bulk_recv.at[0, j],
-                1,
-                tr,
-            ),
-            rcopy(
-                tracer_hbm.at[rows, pl.ds(0, 4)],
-                cext.at[rows, pl.ds(SX + 4, 4)],
-                bulk_send.at[1, j],
-                bulk_recv.at[1, j],
-                -1,
-                tr,
-            ),
-        )
+            out.append(
+                (
+                    rcopy(
+                        outer_s.at[far, rows],
+                        outer_r.at[far, rows],
+                        bulk_send.at[2 + i, j],
+                        bulk_recv.at[2 + i, j],
+                        ds,
+                        tr,
+                    ),
+                    ds,
+                    0,
+                )
+            )
+        return out
+
+    def start_bulk(lo, hi):
+        for ds in (1, -1):
+
+            def body():
+                for j in range(lo, hi):
+                    for c, d, _ in bulks[j]:
+                        if d == ds:
+                            c.start()
+
+            where_there(ds, 0, body)
 
     def shifted(step, buf, q, y):
         ex, ey, ez = DIRS[q]
@@ -275,13 +410,27 @@
         rho, u = moments(f)
         keep_post(0, y, collide(f, rho, u))
 
-    pl.semaphore_wait(barrier, len(peers))
+    pl.semaphore_wait(
+        barrier,
+        n_tracer - 1
+        + n_tracer * (along_x[-1].astype(jnp.int32) + along_x[1].astype(jnp.int32)),
+    )
     first = messages(0)
-    for c in first:
-        c.start()
-    sent_bulk = [bulk(j) for j in range(CHUNKS)]
-    for c in sent_bulk[0]:
-        c.start()
+    start(first)
+
+    load_tracer.wait()
+
+    def round_outer(t, carry):
+        for x in range(2):
+            outer_s[1, t, x] = cext[t, 4 + 2 + x].astype(jnp.bfloat16)
+            outer_s[0, t, x] = cext[t, 4 + SX - 4 + x].astype(jnp.bfloat16)
+        return carry
+
+    lax.fori_loop(0, group, round_outer, 0)
+    bulks = [bulk(j) for j in range(CHUNKS)]
+    start_bulk(0, FIRST)
+    for c in scalars:
+        c.wait()
 
     yi16 = lax.broadcasted_iota(jnp.int32, (NY, NZ), 0)
     zi16 = lax.broadcasted_iota(jnp.int32, (NY, NZ), 1)
@@ -299,34 +448,25 @@
 
     lax.fori_loop(0, group, emit, 0)
 
-    for c in first:
-        c.wait_recv()
-
-    has_x = (
-        jnp.where(sp > 0, 1.0, 0.0).astype(F32),
-        jnp.where(sp < n_space - 1, 1.0, 0.0).astype(F32),
-    )
-    has_y = (
-        jnp.where(tr > 0, 1.0, 0.0).astype(F32),
-        jnp.where(tr < n_tracer - 1, 1.0, 0.0).astype(F32),
-    )
+    arrive(first)
+
     for y in range(TY):
         mine = fluid_v[y]
         for q in range(1, 19):
             ex, ey, ez = DIRS[q]
             yy = y - ey
             if yy < 0:
-                v = yr[0, 0, FLAG] * has_y[0]
+                v = yr[0, 0, FLAG]
             elif yy >= TY:
-                v = yr[0, 1, FLAG] * has_y[1]
+                v = yr[0, 1, FLAG]
             else:
                 v = fluid_v[yy]
             if ex != 0:
                 side = 0 if ex == 1 else 1
                 if 0 <= yy < TY:
-                    row = xr[0, side, FLAG, yy : yy + 1, :] * has_x[side]
+                    row = xr[0, side, FLAG, yy : yy + 1, :]
                 else:
-                    row = cr[0, CORNER_OF[q], 1, 0:1, :] * (has_x[side] * has_y[0 if yy < 0 else 1])
+                    row = cr[0, CORNER_OF[q], 1, 0:1, :]
                 v = pltpu.roll(v, 1 if ex == 1 else SX - 1, 0)
                 v = jnp.where(xi == (0 if ex == 1 else SX - 1), row, v)
             if ez != 0:
@@ -339,12 +479,58 @@
         rho, u = moments(f)
         keep_post(1, y, collide(f, rho, u))
     second = messages(1)
-    for c in second:
-        c.start()
-    for c in sent_bulk[1]:
-        c.start()
-    for c in second:
-        c.wait_recv()
+    start(second)
+    start_bulk(FIRST, SECOND)
+
+    def limited(below, above):
+        return 0.5 * jnp.minimum(
+            jnp.maximum(below, jnp.minimum(above, 0.0)), jnp.maximum(above, 0.0)
+        )
+
+    def states(c, axis, size, index):
+        above = jnp.where(index == size - 1, 0.0, pltpu.roll(c, size - 1, axis)) - c
+        below = c - jnp.where(index == 0, 0.0, pltpu.roll(c, 1, axis))
+        h = limited(below, above)
+        return c + h, pltpu.roll(c - h, size - 1, axis)
+
+    def reaction(t):
+        before = jnp.maximum(t - 1, 0)
+        return before, jnp.where(lax.rem(t, 2) == 1, decay_ref[before], 0.0), decay_ref[t]
+
+    def prepare(j, carry):
+        arrive(bulk(j))
+
+        def one(i, carry):
+            t = j * piece + i
+            before, gain, rate = reaction(t)
+
+            def row(x):
+                if x < 2:
+                    return outer_r[0, t, x].astype(F32)
+                if x >= SX + 6:
+                    return outer_r[1, t, x - SX - 6].astype(F32)
+                return cext[t, x]
+
+            c = row(1)
+            below = c - row(0)
+            for x in range(1, SX + 7):
+                above_c = row(x + 1)
+                above = above_c - c
+                h = limited(below, above)
+                lx[t, x - 1] = c + h
+                hx[t, x - 1] = c - h
+                if 2 <= x < SX + 6:
+                    r = x - 2
+                    ly[t, r], hy[t, r] = states(c, 0, NY, yi16)
+                    lz[t, r], hz[t, r] = states(c, 1, NZ, zi16)
+                    base[t, r] = c + (gain * cext[before, x] - rate * c + emis[t, r])
+                c, below = above_c, above
+            return carry
+
+        return lax.fori_loop(0, piece, one, carry)
+
+    lax.fori_loop(0, FIRST, prepare, 0)
+    arrive(second)
 
     for y in range(TY):
         f = stream(1, y)
@@ -357,61 +543,57 @@
     for x in range(SX):
         fb[tr, 3 + x] = flow_f[x * 4 * TY : (x + 1) * 4 * TY, :].astype(jnp.bfloat16)
 
-    def flow_messages():
-        out = []
-        for ds in (0, 1, -1):
-            for k in range(n_tracer):
-                if (ds, k) == (0, 0):
-                    continue
-                if ds == 0:
-                    src, dst, kind = pl.ds(3, SX), pl.ds(3, SX), 0
-                elif ds == 1:
-                    src, dst, kind = pl.ds(SX, 3), pl.ds(0, 3), 1
-                else:
-                    src, dst, kind = pl.ds(3, 3), pl.ds(SX + 3, 3), 2
-                out.append(
-                    rcopy(
-                        fb.at[tr, src],
-                        fb.at[tr, dst],
-                        flow_send.at[kind, k],
-                        flow_recv.at[kind, tr],
-                        ds,
-                        trs[k],
-                    )
-                )
-        return out
-
-    def flow_arrivals():
-        out = []
-        for kind, rows in ((0, pl.ds(3, SX)), (1, pl.ds(0, 3)), (2, pl.ds(SX + 3, 3))):
-            for k in range(n_tracer):
-                if (kind, k) == (0, 0):
-                    continue
-                t = trs[k]
-                out.append(
-                    rcopy(
-                        fb.at[t, rows],
-                        fb.at[t, rows],
-                        flow_send.at[kind, k],
-                        flow_recv.at[kind, t],
-                        1,
-                        t,
-                    )
-                )
-        return out
-
-    flows = flow_messages()
-    for c in flows:
-        c.start()
+    kinds = {
+        0: (0, pl.ds(3, SX), pl.ds(3, SX)),
+        1: (1, pl.ds(SX, 3), pl.ds(0, 3)),
+        -1: (2, pl.ds(3, 3), pl.ds(SX + 3, 3)),
+    }
+
+    def flow_messages(ds):
+        kind, src, dst = kinds[ds]
+        return [
+            rcopy(
+                fb.at[tr, src],
+                fb.at[tr, dst],
+                flow_send.at[kind, k],
+                flow_recv.at[kind, tr],
+                ds,
+                trs[k],
+            )
+            for k in range(n_tracer)
+            if (ds, k) != (0, 0)
+        ]
+
+    def flow_arrivals(ds):
+        kind, _, rows = kinds[ds]
+        return [
+            rcopy(
+                fb.at[trs[k], rows],
+                fb.at[trs[k], rows],
+                flow_send.at[kind, k],
+                flow_recv.at[kind, trs[k]],
+                1,
+                trs[k],
+            )
+            for k in range(n_tracer)
+            if (ds, k) != (0, 0)
+        ]
+
+    def each(copies, what):
+        def body():
+            for c in copies:
+                getattr(c, what)()
+
+        return body
+
+    flows = {ds: flow_messages(ds) for ds in (1, -1, 0)}
+    for ds in (1, -1, 0):
+        where_there(ds, 0, each(flows[ds], "start"))
     third = messages(2)
-    for c in third:
-        c.start()
-    for j in range(2, CHUNKS):
-        for c in sent_bulk[j]:
-            c.start()
-    load_tracer.wait()
-    for c in flow_arrivals():
-        c.wait_recv()
+    start(third)
+    start_bulk(SECOND, CHUNKS)
+    lax.fori_loop(FIRST, CHUNKS, prepare, 0)
+    where_there(0, 0, each(flow_arrivals(0), "wait_recv"))
 
     def widen(x, carry):
         for t in range(n_tracer):
@@ -419,18 +601,6 @@
             for a in range(4):
                 gflow[a, x, t * TY : (t + 1) * TY, :] = v[a * TY : (a + 1) * TY, :]
         return carry
-
-    lax.fori_loop(0, SX + 6, widen, 0)
-
-    @pl.when(sp == 0)
-    def _():
-        for x in range(3):
-            gflow[3, x] = jnp.zeros((NY, NZ), F32)
-
-    @pl.when(sp == n_space - 1)
-    def _():
-        for x in range(SX + 3, SX + 6):
-            gflow[3, x] = jnp.zeros((NY, NZ), F32)
 
     def split(ref, i, s):
         ref[0, i] = jnp.maximum(s, 0.0)
@@ -443,8 +613,6 @@
             0.5 * (gflow[0, i] + gflow[0, i + 1]) * gflow[3, i] * gflow[3, i + 1],
         )
         return carry
-
-    lax.fori_loop(0, SX + 5, faces_x, 0)
 
     def faces_yz(i, carry):
         air = gflow[3, i + 1]
@@ -456,124 +624,113 @@
         split(face_z, i, jnp.where(zi16 == NZ - 1, 0.0, s))
         return carry
 
-    lax.fori_loop(0, SX + 4, faces_yz, 0)
-
-    def limited(below, above):
-        return 0.5 * jnp.minimum(
-            jnp.maximum(below, jnp.minimum(above, 0.0)), jnp.maximum(above, 0.0)
-        )
-
-    def along_axis(c, axis, size, index, up, down):
-        above = jnp.where(index == size - 1, 0.0, pltpu.roll(c, size - 1, axis)) - c
-        below = c - jnp.where(index == 0, 0.0, pltpu.roll(c, 1, axis))
-        h = limited(below, above)
-        flux = up * (c + h) + down * pltpu.roll(c - h, size - 1, axis)
+    lax.fori_loop(3, SX + 3, widen, 0)
+    lax.fori_loop(3, SX + 2, faces_x, 0)
+    lax.fori_loop(2, SX + 2, faces_yz, 0)
+    for ds in (1, -1):
+        where_there(-ds, 0, each(flow_arrivals(ds), "wait_recv"))
+    lax.fori_loop(0, 3, widen, 0)
+    lax.fori_loop(SX + 3, SX + 6, widen, 0)
+    lax.fori_loop(0, 3, faces_x, 0)
+    lax.fori_loop(SX + 2, SX + 5, faces_x, 0)
+    lax.fori_loop(0, 2, faces_yz, 0)
+    lax.fori_loop(SX + 2, SX + 4, faces_yz, 0)
+
+    def flux_change(faces, i, left, right, axis):
+        flux = faces[0, i] * left + faces[1, i] * right
         return flux - pltpu.roll(flux, 1, axis)
 
-    def section(src, t, rows, face_shift, yz_shift, emit_shift, store):
-        rate = decay_ref[t]
-        before = jnp.maximum(t - 1, 0)
-        gain = jnp.where(lax.rem(t, 2) == 1, decay_ref[before], 0.0)
-        below = src[t, 1] - src[t, 0]
-        flux_low = None
-        left_low = None
-        for j in range(1, rows + 3):
-            c = src[t, j]
-            above = src[t, j + 1] - c
-            h = limited(below, above)
-            if j >= 2:
-                f = j - 1 + face_shift
-                flux = face_x[0, f] * left_low + face_x[1, f] * (c - h)
-                if j >= 3:
-                    r = j - 3
-                    mid = src[t, j - 1]
-                    div = flux - flux_low
-                    i = r + yz_shift
-                    div = div + along_axis(mid, 0, NY, yi16, face_y[0, i], face_y[1, i])
-                    div = div + along_axis(mid, 1, NZ, zi16, face_z[0, i], face_z[1, i])
-                    made = gain * src[before, j - 1] - rate * mid
-                    store(r, mid + (made - div + emis[t, r + emit_shift]))
-                flux_low = flux
-            left_low = c + h
-            below = above
-
-    def section_one(j, carry):
-        for c in bulk(j):
-            c.wait_recv()
-
-        def clear(rows):
-            def body(t, carry):
-                for x in rows:
-                    cext[j * piece + t, x] = jnp.zeros((NY, NZ), F32)
-                return carry
-
-            lax.fori_loop(0, piece, body, 0)
-
-        @pl.when(sp == 0)
-        def _():
-            clear(range(4))
-
-        @pl.when(sp == n_space - 1)
-        def _():
-            clear(range(SX + 4, SX + 8))
-
-        def one(i, carry):
-            t = j * piece + i
-
-            def store(r, v):
-                csec[t, r] = v
-
-            section(cext, t, SX + 4, -1, 0, 0, store)
-            return carry
-
-        return lax.fori_loop(0, piece, one, carry)
-
-    lax.fori_loop(0, CHUNKS, section_one, 0)
+    def section_one(t, carry):
+        low = None
+        for f in range(SX + 5):
+            flux = face_x[0, f] * lx[t, f] + face_x[1, f] * hx[t, f + 1]
+            if f > 0:
+                r = f - 1
+                div = flux - low
+                div = div + flux_change(face_y, r, ly[t, r], hy[t, r], 0)
+                div = div + flux_change(face_z, r, lz[t, r], hz[t, r], 1)
+                csec[t, r] = base[t, r] - div
+            low = flux
+        return carry
+
+    lax.fori_loop(0, group, section_one, 0)
 
     for x in range(SX):
         part[x] = jnp.zeros((NY, NZ), F32)
 
-    def section_two(t, carry):
+    def section_two(t, lo, hi):
+        before, gain, rate = reaction(t)
         weight = coeff_ref[t]
-
-        def store(r, v):
-            cout[t, r] = v
-            part[r] = part[r] + weight * v
-
-        section(csec, t, SX, 1, 2, 2, store)
+        c = csec[t, lo + 1]
+        below = c - csec[t, lo]
+        left = low = None
+        for x in range(lo - 1, hi + 1):
+            above_c = csec[t, x + 3]
+            above = above_c - c
+            h = limited(below, above)
+            if left is not None:
+                flux = face_x[0, x + 2] * left + face_x[1, x + 2] * (c - h)
+                if low is not None:
+                    r = x - 1
+                    mid = csec[t, r + 2]
+                    div = flux - low
+                    i = r + 2
+                    div = div + flux_change(face_y, i, *states(mid, 0, NY, yi16), 0)
+                    div = div + flux_change(face_z, i, *states(mid, 1, NZ, zi16), 1)
+                    made = gain * csec[before, i] - rate * mid
+                    v = mid + (made - div + emis[t, i])
+                    cout[t, r] = v
+                    part[r] = part[r] + weight * v
+                low = flux
+            left = c + h
+            c, below = above_c, above
+
+    def boundary_rows(t, carry):
+        section_two(t, 0, 1)
+        section_two(t, SX - 1, SX)
         return carry
 
-    lax.fori_loop(0, group, section_two, 0)
-    save_tracer = pltpu.make_async_copy(cout, tracer_out, out_sem.at[0])
-    save_tracer.start()
-
-    for x in range(SX):
+    def inner_rows(t, carry):
+        section_two(t, 1, SX - 1)
+        return carry
+
+    def pack(x):
         v = part[x]
         for t in range(n_tracer):
             sb[t, x * 8 : (x + 1) * 8, :] = pltpu.roll(v, (1 - TY * t) % NY, 0)[0:8]
-    buoy = []
+
+    lax.fori_loop(0, group, boundary_rows, 0)
+    pack(0)
+    pack(SX - 1)
+    sides = {}
     for ds, rows, dst in ((1, pl.ds((SX - 1) * 8, 8), 0), (-1, pl.ds(0, 8), 1)):
-        for k in range(n_tracer):
-            buoy.append(
-                rcopy(
-                    sb.at[trs[k], rows],
-                    rx.at[dst, k],
-                    buoy_send.at[dst + 1, k],
-                    buoy_recv.at[dst + 1, k],
-                    ds,
-                    trs[k],
-                )
+        sides[ds] = [
+            rcopy(
+                sb.at[trs[k], rows],
+                rx.at[dst, k],
+                buoy_send.at[dst + 1, k],
+                buoy_recv.at[dst + 1, k],
+                ds,
+                trs[k],
             )
-    for k in range(1, n_tracer):
-        buoy.append(
-            rcopy(sb.at[trs[k]], rb.at[k], buoy_send.at[0, k], buoy_recv.at[0, k], 0, trs[k])
-        )
-    for c in buoy:
-        c.start()
-    for c in third:
-        c.wait_recv()
-    for c in buoy:
-        c.wait_recv()
+            for k in range(n_tracer)
+        ]
+        where_there(ds, 0, each(sides[ds], "start"))
+    lax.fori_loop(0, group, inner_rows, 0)
+    for x in range(1, SX - 1):
+        pack(x)
+    buoy = [
+        rcopy(sb.at[trs[k]], rb.at[k], buoy_send.at[0, k], buoy_recv.at[0, k], 0, trs[k])
+        for k in range(1, n_tracer)
+    ]
+    each(buoy, "start")()
+    save_tracer = pltpu.make_async_copy(cout, tracer_out, out_sem.at[0])
+    save_tracer.start()
+
+    arrive(third)
+    for ds in (1, -1):
+        where_there(-ds, 0, each(sides[ds], "wait_recv"))
+    each(buoy, "wait_recv")()
 
     buf = 0
     for yy in range(-1, TY + 1):
@@ -610,11 +767,14 @@
     save_pop.start()
     save_vel.start()
 
-    for c in first + second + third + flows + buoy:
-        c.wait_send()
-    for pair in sent_bulk:
-        for c in pair:
-            c.wait_send()
+    leave(first + second + third)
+    for j in range(CHUNKS):
+        leave(bulks[j])
+    for ds in (1, -1, 0):
+        where_there(ds, 0, each(flows[ds], "wait_send"))
+    for ds in (1, -1):
+        where_there(ds, 0, each(sides[ds], "wait_send"))
+    each(buoy, "wait_send")()
     save_tracer.wait()
     save_pop.wait()
     save_vel.wait()
@@ -633,7 +793,7 @@
 ):
     group = tracers.shape[0]
     rows = SX * TY
-    smem = pl.BlockSpec(memory_space=pltpu.SMEM)
+    smem = pltpu.SMEM
     hbm = pl.BlockSpec(memory_space=pl.ANY)
     vmem = pltpu.VMEM
     dma = pltpu.SemaphoreType.DMA
@@ -644,9 +804,13 @@
             jax.ShapeDtypeStruct((3 * rows, NZ), F32),
             jax.ShapeDtypeStruct(tracers.shape, F32),
         ),
-        in_specs=[smem] * 4 + [hbm] * 3,
+        in_specs=[hbm] * 7,
         out_specs=(hbm, hbm, hbm),
         scratch_shapes=[
+            smem((group,), F32),
+            smem((group,), F32),
+            smem(source_cells.shape[::-1], jnp.int32),
+            smem(source_rates.shape[::-1], F32),
             vmem((19 * rows, NZ), F32),
             vmem((rows, NZ), jnp.int32),
             vmem((TY, SX, NZ), F32),
@@ -665,6 +829,15 @@
             vmem((2, SX + 4, NY, NZ), F32),
             vmem((2, SX + 4, NY, NZ), F32),
             vmem((group, SX + 8, NY, NZ), F32),
+            vmem((2, group, 2, NY, NZ), jnp.bfloat16),
+            vmem((2, group, 2, NY, NZ), jnp.bfloat16),
+            vmem((group, SX + 6, NY, NZ), F32),
+            vmem((group, SX + 6, NY, NZ), F32),
+            vmem((group, SX + 4, NY, NZ), F32),
+            vmem((group, SX + 4, NY, NZ), F32),
+            vmem((group, SX + 4, NY, NZ), F32),
+            vmem((group, SX + 4, NY, NZ), F32),
+            vmem((group, SX + 4, NY, NZ), F32),
             vmem((group, SX + 4, NY, NZ), F32),
             vmem((group, SX, NY, NZ), F32),
             vmem((group, SX + 4, NY, NZ), F32),
@@ -674,19 +847,19 @@
             vmem((2, n_tracer, 8, NZ), F32),
             vmem((19 * rows, NZ), F32),
             vmem((3 * rows, NZ), F32),
-            dma((3,)),
+            dma((7,)),
             dma((3,)),
             dma((3, 8)),
             dma((3, 8)),
-            dma((2, CHUNKS)),
-            dma((2, CHUNKS)),
+            dma((4, CHUNKS)),
+            dma((4, CHUNKS)),
             dma((3, n_tracer)),
             dma((3, n_tracer)),
             dma((3, n_tracer)),
             dma((3, n_tracer)),
         ],
         compiler_params=pltpu.CompilerParams(
-            collective_id=0, has_side_effects=True, vmem_limit_bytes=40 * 1024 * 1024
+            collective_id=0, has_side_effects=True, vmem_limit_bytes=67043328
         ),
         name="plume",
     )(

time: 66.1 us -> 58.4 us (0.88)
  the two profiles are of different devices: /device:TPU:1 before, /device:TPU:7 now
where the time goes in v2:
time: 58.4 us; the launch traced here: 58.2 us
  Pallas kernels  52.9 us (91%)
  local copies, waits for them, and re-layouts  4.64 us (8%)
  between operations  0.65 us (1%)
    pallas_call x1, Pallas kernels, local(): pl.pallas_call(functools.partial(kernel, n_space, n_tracer), out_shape=(j...  52.9 us
    unnamed x5, local copies, waits for them, and re-layouts  4.64 us

profile of v2, /device:TPU:7, one launch (start us, length us, event | category | flops | bytes accessed | tf_op | source)
XLA Modules:
  0.0 58.2 jit_solution(7761250654662902659)
XLA Ops:
  0.6 52.9 %plume.1 = (f32[608,128]{1,0:T(8,128)}, f32[96,128]{1,0:T(8,128)}, f32[16,8,16,128]{3,2,1,0:T(8,128)}) custom-call(f32[16]{0:T(128)} %decay_hbm.1, f32[16]{0:T(128)} %coeff_hbm.1, s32[8,16]{1,0:T(8,128)} %bitcast.10, f32[8,16]{1,0:T(8,128)} %bitcast.11, f32[608,128]{1,0:T(8,128)} %bitcast.6, s32[32,128]{1,0:T(8,128)} %bitcast.9, f32[16,8,16,128]{3,2,1,0:T(8,128)} %tracer_hbm.1), custom_call_target="tpu_custom_call" | custom-call | tf_op jit(solution)/shard_map/plume/pallas_call | solution.py:800
  53.5 0.0 copy-start
  53.5 1.7 %copy.13 = f32[19,8,4,128]{3,2,1,0:T(4,128)} copy(f32[19,8,4,128]{3,2,1,0:T(4,128)} %bitcast.7) | data formatting | bytes 622592
  55.3 0.0 copy-done
  55.3 0.6 %copy.14 = f32[3,8,4,128]{3,2,1,0:T(4,128)} copy(f32[3,8,4,128]{3,2,1,0:T(4,128)S(1)} %bitcast.8) | data formatting | bytes 98304
  55.9 2.3 %copy.15 = f32[16,8,16,128]{3,2,1,0:T(8,128)} copy(f32[16,8,16,128]{3,2,1,0:T(8,128)} %get-tuple-element.14) | data formatting | bytes 2097152
Async XLA Ops:
  53.5 1.7 %copy-start = (f32[96,128]{1,0:T(8,128)S(1)}, f32[96,128]{1,0:T(8,128)}, u32[]{:S(2)}) copy-start(f32[96,128]{1,0:T(8,128)} %get-tuple-element.7) | copy-start | bytes 147460

commit v3 on v2

--- a/solution.py
+++ b/solution.py
@@ -39,7 +39,8 @@
 SX, NY, NZ = 8, 16, 128
 TY = 4
 CHUNKS = 8
-FIRST, SECOND = 3, 6
+FIRST = 4
+INNER = 5
 F32 = jnp.float32
 
 
@@ -53,9 +54,9 @@
     pop_hbm,
     mask_hbm,
     tracer_hbm,
-    pop_out,
-    vel_out,
-    tracer_out,
+    fout,
+    vout,
+    cout,
     decay_ref,
     coeff_ref,
     cells_ref,
@@ -88,16 +89,12 @@
     hz,
     base,
     csec,
-    cout,
     emis,
     part,
     sb,
     rb,
     rx,
-    fout,
-    vout,
     load_sem,
-    out_sem,
     halo_send,
     halo_recv,
     bulk_send,
@@ -480,16 +477,14 @@
         keep_post(1, y, collide(f, rho, u))
     second = messages(1)
     start(second)
-    start_bulk(FIRST, SECOND)
+    start_bulk(FIRST, CHUNKS)
 
     def limited(below, above):
-        return 0.5 * jnp.minimum(
-            jnp.maximum(below, jnp.minimum(above, 0.0)), jnp.maximum(above, 0.0)
-        )
-
-    def states(c, axis, size, index):
-        above = jnp.where(index == size - 1, 0.0, pltpu.roll(c, size - 1, axis)) - c
-        below = c - jnp.where(index == 0, 0.0, pltpu.roll(c, 1, axis))
+        return jnp.minimum(jnp.maximum(below, jnp.minimum(above, 0.0)), jnp.maximum(above, 0.0))
+
+    def states(c, half, axis, size, index):
+        above = jnp.where(index == size - 1, 0.0, pltpu.roll(half, size - 1, axis)) - half
+        below = half - jnp.where(index == 0, 0.0, pltpu.roll(half, 1, axis))
         h = limited(below, above)
         return c + h, pltpu.roll(c - h, size - 1, axis)
 
@@ -497,12 +492,38 @@
         before = jnp.maximum(t - 1, 0)
         return before, jnp.where(lax.rem(t, 2) == 1, decay_ref[before], 0.0), decay_ref[t]
 
-    def prepare(j, carry):
+    def ready_rows(t, row, lo, hi):
+        half = 0.5 * row(lo)
+        below = half - 0.5 * row(lo - 1)
+        for x in range(lo, hi):
+            above_half = 0.5 * row(x + 1)
+            above = above_half - half
+            h = limited(below, above)
+            c = row(x)
+            lx[t, x - 1] = c + h
+            hx[t, x - 1] = c - h
+            half, below = above_half, above
+
+    def ready_planes(t, rows):
+        before, gain, rate = reaction(t)
+        for x in rows:
+            r = x - 2
+            c = cext[t, x]
+            half = 0.5 * c
+            ly[t, r], hy[t, r] = states(c, half, 0, NY, yi16)
+            lz[t, r], hz[t, r] = states(c, half, 1, NZ, zi16)
+            base[t, r] = c + (gain * cext[before, x] - rate * c + emis[t, r])
+
+    def prepare_own(t, carry):
+        ready_planes(t, range(4, SX + 4))
+        ready_rows(t, lambda x: cext[t, x], 5, SX + 3)
+        return carry
+
+    def prepare_halo(j, carry):
         arrive(bulk(j))
 
         def one(i, carry):
             t = j * piece + i
-            before, gain, rate = reaction(t)
 
             def row(x):
                 if x < 2:
@@ -511,25 +532,14 @@
                     return outer_r[1, t, x - SX - 6].astype(F32)
                 return cext[t, x]
 
-            c = row(1)
-            below = c - row(0)
-            for x in range(1, SX + 7):
-                above_c = row(x + 1)
-                above = above_c - c
-                h = limited(below, above)
-                lx[t, x - 1] = c + h
-                hx[t, x - 1] = c - h
-                if 2 <= x < SX + 6:
-                    r = x - 2
-                    ly[t, r], hy[t, r] = states(c, 0, NY, yi16)
-                    lz[t, r], hz[t, r] = states(c, 1, NZ, zi16)
-                    base[t, r] = c + (gain * cext[before, x] - rate * c + emis[t, r])
-                c, below = above_c, above
+            ready_planes(t, (2, 3, SX + 4, SX + 5))
+            ready_rows(t, row, 1, 5)
+            ready_rows(t, row, SX + 3, SX + 7)
             return carry
 
         return lax.fori_loop(0, piece, one, carry)
 
-    lax.fori_loop(0, FIRST, prepare, 0)
+    lax.fori_loop(0, group, prepare_own, 0)
     arrive(second)
 
     for y in range(TY):
@@ -591,8 +601,7 @@
         where_there(ds, 0, each(flows[ds], "start"))
     third = messages(2)
     start(third)
-    start_bulk(SECOND, CHUNKS)
-    lax.fori_loop(FIRST, CHUNKS, prepare, 0)
+    lax.fori_loop(0, CHUNKS, prepare_halo, 0)
     where_there(0, 0, each(flow_arrivals(0), "wait_recv"))
 
     def widen(x, carry):
@@ -661,37 +670,43 @@
     def section_two(t, lo, hi):
         before, gain, rate = reaction(t)
         weight = coeff_ref[t]
-        c = csec[t, lo + 1]
-        below = c - csec[t, lo]
+        half = 0.5 * csec[t, lo + 1]
+        below = half - 0.5 * csec[t, lo]
         left = low = None
         for x in range(lo - 1, hi + 1):
-            above_c = csec[t, x + 3]
-            above = above_c - c
+            above_half = 0.5 * csec[t, x + 3]
+            above = above_half - half
             h = limited(below, above)
+            c = csec[t, x + 2]
             if left is not None:
                 flux = face_x[0, x + 2] * left + face_x[1, x + 2] * (c - h)
                 if low is not None:
                     r = x - 1
-                    mid = csec[t, r + 2]
+                    i = r + 2
+                    mid = csec[t, i]
+                    mid_half = 0.5 * mid
                     div = flux - low
-                    i = r + 2
-                    div = div + flux_change(face_y, i, *states(mid, 0, NY, yi16), 0)
-                    div = div + flux_change(face_z, i, *states(mid, 1, NZ, zi16), 1)
+                    div = div + flux_change(face_y, i, *states(mid, mid_half, 0, NY, yi16), 0)
+                    div = div + flux_change(face_z, i, *states(mid, mid_half, 1, NZ, zi16), 1)
                     made = gain * csec[before, i] - rate * mid
                     v = mid + (made - div + emis[t, i])
                     cout[t, r] = v
                     part[r] = part[r] + weight * v
                 low = flux
             left = c + h
-            c, below = above_c, above
+            half, below = above_half, above
 
     def boundary_rows(t, carry):
         section_two(t, 0, 1)
         section_two(t, SX - 1, SX)
         return carry
 
-    def inner_rows(t, carry):
-        section_two(t, 1, SX - 1)
+    def lower_rows(t, carry):
+        section_two(t, 1, INNER)
+        return carry
+
+    def upper_rows(t, carry):
+        section_two(t, INNER, SX - 1)
         return carry
 
     def pack(x):
@@ -699,6 +714,24 @@
         for t in range(n_tracer):
             sb[t, x * 8 : (x + 1) * 8, :] = pltpu.roll(v, (1 - TY * t) % NY, 0)[0:8]
 
+    def to_owners(i, lo, hi):
+        rows = pl.ds(lo * 8, (hi - lo) * 8)
+        return [
+            rcopy(
+                sb.at[trs[k], rows],
+                rb.at[k, rows],
+                buoy_send.at[2 + i, k],
+                buoy_recv.at[2 + i, k],
+                0,
+                trs[k],
+            )
+            for k in range(1, n_tracer)
+        ]
+
+    buoy = [
+        to_owners(i, lo, hi)
+        for i, (lo, hi) in enumerate(((0, 1), (SX - 1, SX), (1, INNER), (INNER, SX - 1)))
+    ]
     lax.fori_loop(0, group, boundary_rows, 0)
     pack(0)
     pack(SX - 1)
@@ -708,29 +741,34 @@
             rcopy(
                 sb.at[trs[k], rows],
                 rx.at[dst, k],
-                buoy_send.at[dst + 1, k],
-                buoy_recv.at[dst + 1, k],
+                buoy_send.at[dst, k],
+                buoy_recv.at[dst, k],
                 ds,
                 trs[k],
             )
             for k in range(n_tracer)
         ]
         where_there(ds, 0, each(sides[ds], "start"))
-    lax.fori_loop(0, group, inner_rows, 0)
-    for x in range(1, SX - 1):
+    each(buoy[0] + buoy[1], "start")()
+    lax.fori_loop(0, group, lower_rows, 0)
+    for x in range(1, INNER):
         pack(x)
-    buoy = [
-        rcopy(sb.at[trs[k]], rb.at[k], buoy_send.at[0, k], buoy_recv.at[0, k], 0, trs[k])
-        for k in range(1, n_tracer)
-    ]
-    each(buoy, "start")()
-    save_tracer = pltpu.make_async_copy(cout, tracer_out, out_sem.at[0])
-    save_tracer.start()
-
+    each(buoy[2], "start")()
+    lax.fori_loop(0, group, upper_rows, 0)
+    for x in range(INNER, SX - 1):
+        pack(x)
+    each(buoy[3], "start")()
     arrive(third)
+    leave(first + second + third)
+    for j in range(CHUNKS):
+        leave(bulks[j])
+    for ds in (1, -1, 0):
+        where_there(ds, 0, each(flows[ds], "wait_send"))
+    for ds in (1, -1):
+        where_there(ds, 0, each(sides[ds], "wait_send"))
     for ds in (1, -1):
         where_there(-ds, 0, each(sides[ds], "wait_recv"))
-    each(buoy, "wait_recv")()
+    each([c for row in buoy for c in row], "wait_recv")()
 
     buf = 0
     for yy in range(-1, TY + 1):
@@ -762,22 +800,21 @@
             fout[pl.ds(q * SX * TY + y, SX, stride=TY), :] = f[q]
         for a in range(3):
             vout[pl.ds(a * SX * TY + y, SX, stride=TY), :] = u[a] * fluid_v[y]
-    save_pop = pltpu.make_async_copy(fout, pop_out, out_sem.at[1])
-    save_vel = pltpu.make_async_copy(vout, vel_out, out_sem.at[2])
-    save_pop.start()
-    save_vel.start()
-
-    leave(first + second + third)
-    for j in range(CHUNKS):
-        leave(bulks[j])
-    for ds in (1, -1, 0):
-        where_there(ds, 0, each(flows[ds], "wait_send"))
-    for ds in (1, -1):
-        where_there(ds, 0, each(sides[ds], "wait_send"))
-    each(buoy, "wait_send")()
-    save_tracer.wait()
-    save_pop.wait()
-    save_vel.wait()
+
+    each([c for row in buoy for c in row], "wait_send")()
+
+
+def hand_over(pop_in, vel_in, tracer_in, pop_out, vel_out, tracer_out, sem):
+    copies = [
+        pltpu.make_async_copy(a, b, sem.at[i])
+        for i, (a, b) in enumerate(
+            ((tracer_in, tracer_out), (pop_in, pop_out), (vel_in, vel_out))
+        )
+    ]
+    for c in copies:
+        c.start()
+    for c in copies:
+        c.wait()
 
 
 def local(
@@ -800,12 +837,12 @@
     out = pl.pallas_call(
         functools.partial(kernel, n_space, n_tracer),
         out_shape=(
-            jax.ShapeDtypeStruct((19 * rows, NZ), F32),
-            jax.ShapeDtypeStruct((3 * rows, NZ), F32),
-            jax.ShapeDtypeStruct(tracers.shape, F32),
+            vmem((19 * rows, NZ), F32),
+            vmem((3 * rows, NZ), F32),
+            vmem(tracers.shape, F32),
         ),
-        in_specs=[hbm] * 7,
-        out_specs=(hbm, hbm, hbm),
+        in_specs=[pl.BlockSpec(memory_space=pltpu.HBM)] * 7,
+        out_specs=(pl.BlockSpec(memory_space=pltpu.VMEM),) * 3,
         scratch_shapes=[
             smem((group,), F32),
             smem((group,), F32),
@@ -839,27 +876,23 @@
             vmem((group, SX + 4, NY, NZ), F32),
             vmem((group, SX + 4, NY, NZ), F32),
             vmem((group, SX + 4, NY, NZ), F32),
-            vmem((group, SX, NY, NZ), F32),
             vmem((group, SX + 4, NY, NZ), F32),
             vmem((SX, NY, NZ), F32),
             vmem((n_tracer, SX * 8, NZ), F32),
             vmem((n_tracer, SX * 8, NZ), F32),
             vmem((2, n_tracer, 8, NZ), F32),
-            vmem((19 * rows, NZ), F32),
-            vmem((3 * rows, NZ), F32),
             dma((7,)),
-            dma((3,)),
             dma((3, 8)),
             dma((3, 8)),
             dma((4, CHUNKS)),
             dma((4, CHUNKS)),
             dma((3, n_tracer)),
             dma((3, n_tracer)),
-            dma((3, n_tracer)),
-            dma((3, n_tracer)),
+            dma((6, n_tracer)),
+            dma((6, n_tracer)),
         ],
         compiler_params=pltpu.CompilerParams(
-            collective_id=0, has_side_effects=True, vmem_limit_bytes=67043328
+            collective_id=0, has_side_effects=True, vmem_limit_bytes=65400000
         ),
         name="plume",
     )(
@@ -871,6 +904,15 @@
         solid_mask.reshape(rows, NZ),
         tracers,
     )
+    out = pl.pallas_call(
+        hand_over,
+        out_shape=tuple(jax.ShapeDtypeStruct(v.shape, v.dtype) for v in out),
+        in_specs=[hbm] * 3,
+        out_specs=(hbm,) * 3,
+        scratch_shapes=[dma((3,))],
+        compiler_params=pltpu.CompilerParams(vmem_limit_bytes=1024 * 1024),
+        name="hand_over",
+    )(*out)
     return (
         out[0].reshape(populations.shape),
         out[1].reshape((3,) + populations.shape[1:]),

time: 58.4 us -> 56 us (0.959)
  the two profiles are of different devices: /device:TPU:7 before, /device:TPU:1 now
where the time goes in v3:
time: 56 us; the launch traced here: 55.8 us
  Pallas kernels  55.2 us (99%)
  between operations  0.64 us (1%)
    pallas_call x1, Pallas kernels, local(): pl.pallas_call(functools.partial(kernel, n_space, n_tracer), out_shape=(v...  54.1 us

profile of v3, /device:TPU:1, one launch (start us, length us, event | category | flops | bytes accessed | tf_op | source)
XLA Modules:
  0.0 55.8 jit_solution(12216366030890511005)
XLA Ops:
  0.6 54.1 %plume.1 = (f32[608,128]{1,0:T(8,128)S(1)}, f32[96,128]{1,0:T(8,128)S(1)}, f32[16,8,16,128]{3,2,1,0:T(8,128)S(1)}) custom-call(f32[16]{0:T(128)} %decay_hbm.1, f32[16]{0:T(128)} %coeff_hbm.1, s32[8,16]{1,0:T(8,128)} %bitcast.8, f32[8,16]{1,0:T(8,128)} %bitcast.9, f32[608,128]{1,0:T(8,128)} %bitcast.6, s32[32,128]{1,0:T(8,128)} %bitcast.7, ...), custom_call_target="tpu_custom_call" | custom-call | tf_op jit(solution)/shard_map/plume/pallas_call | solution.py:837
  54.7 1.1 %hand_over.1 = (f32[608,128]{1,0:T(8,128)}, f32[96,128]{1,0:T(8,128)}, f32[16,8,16,128]{3,2,1,0:T(8,128)}) custom-call(f32[608,128]{1,0:T(8,128)S(1)} %get-tuple-element.9.pop_in, f32[96,128]{1,0:T(8,128)S(1)} %get-tuple-element.10.vel_in, f32[16,8,16,128]{3,2,1,0:T(8,128)S(1)} %get-tuple-element.11.tracer_in), custom_call_target="tpu_custom_call" | custom-call | tf_op jit(solution)/shard_map/hand_over/pallas_call | solution.py:907

commit v4 on v3

--- a/solution.py
+++ b/solution.py
@@ -40,7 +40,6 @@
 TY = 4
 CHUNKS = 8
 FIRST = 4
-INNER = 5
 F32 = jnp.float32
 
 
@@ -604,26 +603,24 @@
     lax.fori_loop(0, CHUNKS, prepare_halo, 0)
     where_there(0, 0, each(flow_arrivals(0), "wait_recv"))
 
-    def widen(x, carry):
+    def widen(x):
         for t in range(n_tracer):
             v = fb[t, x].astype(F32)
             for a in range(4):
                 gflow[a, x, t * TY : (t + 1) * TY, :] = v[a * TY : (a + 1) * TY, :]
-        return carry
 
     def split(ref, i, s):
         ref[0, i] = jnp.maximum(s, 0.0)
         ref[1, i] = jnp.minimum(s, 0.0)
 
-    def faces_x(i, carry):
+    def faces_x(i):
         split(
             face_x,
             i,
             0.5 * (gflow[0, i] + gflow[0, i + 1]) * gflow[3, i] * gflow[3, i + 1],
         )
-        return carry
-
-    def faces_yz(i, carry):
+
+    def faces_yz(i):
         air = gflow[3, i + 1]
         v = gflow[1, i + 1]
         s = 0.5 * (v + pltpu.roll(v, NY - 1, 0)) * air * pltpu.roll(air, NY - 1, 0)
@@ -631,59 +628,55 @@
         v = gflow[2, i + 1]
         s = 0.5 * (v + pltpu.roll(v, NZ - 1, 1)) * air * pltpu.roll(air, NZ - 1, 1)
         split(face_z, i, jnp.where(zi16 == NZ - 1, 0.0, s))
-        return carry
-
-    lax.fori_loop(3, SX + 3, widen, 0)
-    lax.fori_loop(3, SX + 2, faces_x, 0)
-    lax.fori_loop(2, SX + 2, faces_yz, 0)
-    for ds in (1, -1):
-        where_there(-ds, 0, each(flow_arrivals(ds), "wait_recv"))
-    lax.fori_loop(0, 3, widen, 0)
-    lax.fori_loop(SX + 3, SX + 6, widen, 0)
-    lax.fori_loop(0, 3, faces_x, 0)
-    lax.fori_loop(SX + 2, SX + 5, faces_x, 0)
-    lax.fori_loop(0, 2, faces_yz, 0)
-    lax.fori_loop(SX + 2, SX + 4, faces_yz, 0)
-
+
+    for i in range(3, SX + 3):
+        widen(i)
+    for i in range(3, SX + 2):
+        faces_x(i)
+    for i in range(2, SX + 2):
+        faces_yz(i)
     def flux_change(faces, i, left, right, axis):
         flux = faces[0, i] * left + faces[1, i] * right
         return flux - pltpu.roll(flux, 1, axis)
 
-    def section_one(t, carry):
+    def section_one(t, lo, hi):
         low = None
-        for f in range(SX + 5):
+        rows = {}
+        for f in range(lo, hi + 1):
             flux = face_x[0, f] * lx[t, f] + face_x[1, f] * hx[t, f + 1]
-            if f > 0:
+            if f > lo:
                 r = f - 1
                 div = flux - low
                 div = div + flux_change(face_y, r, ly[t, r], hy[t, r], 0)
                 div = div + flux_change(face_z, r, lz[t, r], hz[t, r], 1)
-                csec[t, r] = base[t, r] - div
+                rows[r] = base[t, r] - div
+                csec[t, r] = rows[r]
             low = flux
-        return carry
-
-    lax.fori_loop(0, group, section_one, 0)
+        return rows
 
     for x in range(SX):
         part[x] = jnp.zeros((NY, NZ), F32)
 
-    def section_two(t, lo, hi):
+    def section_two(t, lo, hi, rows):
+        def at(r):
+            return rows[r] if r in rows else csec[t, r]
+
         before, gain, rate = reaction(t)
         weight = coeff_ref[t]
-        half = 0.5 * csec[t, lo + 1]
-        below = half - 0.5 * csec[t, lo]
+        half = 0.5 * at(lo + 1)
+        below = half - 0.5 * at(lo)
         left = low = None
         for x in range(lo - 1, hi + 1):
-            above_half = 0.5 * csec[t, x + 3]
+            above_half = 0.5 * at(x + 3)
             above = above_half - half
             h = limited(below, above)
-            c = csec[t, x + 2]
+            c = at(x + 2)
             if left is not None:
                 flux = face_x[0, x + 2] * left + face_x[1, x + 2] * (c - h)
                 if low is not None:
                     r = x - 1
                     i = r + 2
-                    mid = csec[t, i]
+                    mid = at(i)
                     mid_half = 0.5 * mid
                     div = flux - low
                     div = div + flux_change(face_y, i, *states(mid, mid_half, 0, NY, yi16), 0)
@@ -696,17 +689,29 @@
             left = c + h
             half, below = above_half, above
 
-    def boundary_rows(t, carry):
-        section_two(t, 0, 1)
-        section_two(t, SX - 1, SX)
+    def in_pairs(body):
+        def pair(i, carry):
+            body(2 * i, carry)
+            body(2 * i + 1, carry)
+            return carry
+
+        lax.fori_loop(0, group // 2, pair, 0)
+
+    def middle(t, carry):
+        section_two(t, 3, SX - 3, section_one(t, 3, SX + 1))
         return carry
 
-    def lower_rows(t, carry):
-        section_two(t, 1, INNER)
+    def outer(t, carry):
+        section_two(t, 0, 1, section_one(t, 0, 3))
+        section_two(t, SX - 1, SX, section_one(t, SX + 1, SX + 4))
         return carry
 
-    def upper_rows(t, carry):
-        section_two(t, INNER, SX - 1)
+    def lower(t, carry):
+        section_two(t, 1, 3, {})
+        return carry
+
+    def upper(t, carry):
+        section_two(t, SX - 3, SX - 1, {})
         return carry
 
     def pack(x):
@@ -730,9 +735,28 @@
 
     buoy = [
         to_owners(i, lo, hi)
-        for i, (lo, hi) in enumerate(((0, 1), (SX - 1, SX), (1, INNER), (INNER, SX - 1)))
+        for i, (lo, hi) in enumerate(((3, SX - 3), (0, 1), (SX - 1, SX), (1, 3), (SX - 3, SX - 1)))
     ]
-    lax.fori_loop(0, group, boundary_rows, 0)
+    in_pairs(middle)
+    for x in range(3, SX - 3):
+        pack(x)
+    each(buoy[0], "start")()
+    for ds in (1, -1):
+        where_there(-ds, 0, each(flow_arrivals(ds), "wait_recv"))
+    for i in range(0, 3):
+        widen(i)
+    for i in range(SX + 3, SX + 6):
+        widen(i)
+    for i in range(0, 3):
+        faces_x(i)
+    for i in range(SX + 2, SX + 5):
+        faces_x(i)
+    for i in range(0, 2):
+        faces_yz(i)
+    for i in range(SX + 2, SX + 4):
+        faces_yz(i)
+
+    in_pairs(outer)
     pack(0)
     pack(SX - 1)
     sides = {}
@@ -749,15 +773,15 @@
             for k in range(n_tracer)
         ]
         where_there(ds, 0, each(sides[ds], "start"))
-    each(buoy[0] + buoy[1], "start")()
-    lax.fori_loop(0, group, lower_rows, 0)
-    for x in range(1, INNER):
-        pack(x)
-    each(buoy[2], "start")()
-    lax.fori_loop(0, group, upper_rows, 0)
-    for x in range(INNER, SX - 1):
+    each(buoy[1] + buoy[2], "start")()
+    in_pairs(lower)
+    for x in (1, 2):
         pack(x)
     each(buoy[3], "start")()
+    in_pairs(upper)
+    for x in (SX - 3, SX - 2):
+        pack(x)
+    each(buoy[4], "start")()
     arrive(third)
     leave(first + second + third)
     for j in range(CHUNKS):
@@ -805,12 +829,11 @@
 
 
 def hand_over(pop_in, vel_in, tracer_in, pop_out, vel_out, tracer_out, sem):
-    copies = [
-        pltpu.make_async_copy(a, b, sem.at[i])
-        for i, (a, b) in enumerate(
-            ((tracer_in, tracer_out), (pop_in, pop_out), (vel_in, vel_out))
-        )
-    ]
+    part = tracer_in.shape[0] // 4
+    pairs = [(a.at[pl.ds(i * part, part)], b.at[pl.ds(i * part, part)])
+             for a, b in ((tracer_in, tracer_out),) for i in range(4)]
+    pairs += [(pop_in, pop_out), (vel_in, vel_out)]
+    copies = [pltpu.make_async_copy(a, b, sem.at[i]) for i, (a, b) in enumerate(pairs)]
     for c in copies:
         c.start()
     for c in copies:
@@ -888,8 +911,8 @@
             dma((4, CHUNKS)),
             dma((3, n_tracer)),
             dma((3, n_tracer)),
-            dma((6, n_tracer)),
-            dma((6, n_tracer)),
+            dma((7, n_tracer)),
+            dma((7, n_tracer)),
         ],
         compiler_params=pltpu.CompilerParams(
             collective_id=0, has_side_effects=True, vmem_limit_bytes=65400000
@@ -909,7 +932,7 @@
         out_shape=tuple(jax.ShapeDtypeStruct(v.shape, v.dtype) for v in out),
         in_specs=[hbm] * 3,
         out_specs=(hbm,) * 3,
-        scratch_shapes=[dma((3,))],
+        scratch_shapes=[dma((6,))],
         compiler_params=pltpu.CompilerParams(vmem_limit_bytes=1024 * 1024),
         name="hand_over",
     )(*out)

time: 56 us -> 51.9 us (0.927)
  Pallas kernels: 55.2 us -> 51.1 us
    pallas_call x1, Pallas kernels: 54.1 us -> 50 us  [local(): pl.pallas_call(functools.partial(kernel, n_space, n_tracer), out_shape=(v...]
where the time goes in v4:
time: 51.9 us; the launch traced here: 51.8 us
  Pallas kernels  51.1 us (98%)
  between operations  0.64 us (1%)
    pallas_call x1, Pallas kernels, local(): pl.pallas_call(functools.partial(kernel, n_space, n_tracer), out_shape=(v...  50 us
    pallas_call x1, Pallas kernels, local(): pl.pallas_call(hand_over, out_shape=tuple((jax.ShapeDtypeStruct(v.shape,...  1.12 us

profile of v4, /device:TPU:1, one launch (start us, length us, event | category | flops | bytes accessed | tf_op | source)
XLA Modules:
  0.0 51.8 jit_solution(2402680912729966946)
XLA Ops:
  0.6 50.0 %plume.1 = (f32[608,128]{1,0:T(8,128)S(1)}, f32[96,128]{1,0:T(8,128)S(1)}, f32[16,8,16,128]{3,2,1,0:T(8,128)S(1)}) custom-call(f32[16]{0:T(128)} %decay_hbm.1, f32[16]{0:T(128)} %coeff_hbm.1, s32[8,16]{1,0:T(8,128)} %bitcast.8, f32[8,16]{1,0:T(8,128)} %bitcast.9, f32[608,128]{1,0:T(8,128)} %bitcast.6, s32[32,128]{1,0:T(8,128)} %bitcast.7, ...), custom_call_target="tpu_custom_call" | custom-call | tf_op jit(solution)/shard_map/plume/pallas_call | solution.py:860
  50.6 1.1 %hand_over.1 = (f32[608,128]{1,0:T(8,128)}, f32[96,128]{1,0:T(8,128)}, f32[16,8,16,128]{3,2,1,0:T(8,128)}) custom-call(f32[608,128]{1,0:T(8,128)S(1)} %get-tuple-element.9.pop_in, f32[96,128]{1,0:T(8,128)S(1)} %get-tuple-element.10.vel_in, f32[16,8,16,128]{3,2,1,0:T(8,128)S(1)} %get-tuple-element.11.tracer_in), custom_call_target="tpu_custom_call" | custom-call | tf_op jit(solution)/shard_map/hand_over/pallas_call | solution.py:930
